TPU v7x, 32 devices: a whole 2x2x4 slice. The times are simulated.
32 devices in a mesh: row: 4 (over z), col: 4 (over x, core), layer: 2 (over y).
Axes of the slice: x: 2, y: 2, z: 4, core: 2. Of those that a mesh axis runs over, the one named last changes fastest.
Arguments:
- intersection: bfloat16 [2048, 2, 1024], P('row', 'layer', 'col'), may hold values from -6 to 6
- density: bfloat16 [2, 1024, 2, 1024], P('layer', 'row', None, 'col'), may hold values from -0.125 to 0.125
- hamiltonian: bfloat16 [2, 1024, 2, 1024], P('layer', 'row', None, 'col'), may hold values from -0.125 to 0.125
- intersection_pattern: int32 [16, 2, 8], P('row', 'layer', 'col'), may hold values 0 or 1
- density_pattern: int32 [2, 8, 2, 8], P('layer', 'row', None, 'col'), may hold values 0 or 1
- hamiltonian_pattern: int32 [2, 8, 2, 8], P('layer', 'row', None, 'col'), may hold values 0 or 1
- product_filter: int32 [16, 2, 8], P('row', 'layer', 'col'), may hold values 0 or 1
Outputs:
- gradient_term: bfloat16 [2048, 2, 1024], P('row', 'layer', 'col')
All inputs are finite; a program needn't handle non-finite values. No bound on the sum of `intersection_pattern` or of `density_pattern` or of `hamiltonian_pattern` or of `product_filter` on one device may be relied on, other than what follows from the above.
Results may differ from a plain program's by a relative error of at most 0.005.
Values may be sent and summed in bfloat16 or wider, within the bound.
No kernel may reach another device: no remote copies, remote signals or barrier semaphores. Data moves between devices by JAX's collectives and lax.ppermute only.
A program may use at most 64 MiB of HBM per device.

v0:
```python
import jax
import jax.numpy as jnp
from jax import lax
from jax.sharding import PartitionSpec as P


def mask_left(block_tile, pattern):
    row_count, _, col_count = block_tile.shape
    row_blocks = pattern.shape[0]
    col_blocks = pattern.shape[2]
    blocks = block_tile.reshape(
        row_blocks, row_count // row_blocks, col_blocks, col_count // col_blocks
    )
    blocks = blocks * pattern.reshape(row_blocks, 1, col_blocks, 1).astype(jnp.bfloat16)
    return blocks.reshape(row_count, col_count)


def mask_right(block_tile, pattern):
    _, row_count, layers, col_count = block_tile.shape
    row_blocks = pattern.shape[1]
    col_blocks = pattern.shape[3]
    blocks = block_tile.reshape(
        row_blocks, row_count // row_blocks, layers, col_blocks, col_count // col_blocks
    )
    blocks = blocks * pattern.reshape(row_blocks, 1, layers, col_blocks, 1).astype(jnp.bfloat16)
    return blocks.reshape(row_count, layers * col_count)


def multiply(left_tile, right_tile):
    whole_left = lax.all_gather(left_tile, "col", axis=1, tiled=True)
    row_count = whole_left.shape[0]
    layers = lax.axis_size("layer")
    column_span = right_tile.shape[1] // layers
    partial_value = jnp.dot(
        whole_left,
        lax.all_gather(right_tile, "row", axis=0, tiled=True),
        preferred_element_type=jnp.float32,
    )
    return lax.psum_scatter(
        partial_value.reshape(row_count, layers, column_span),
        "layer",
        scatter_dimension=1,
        tiled=True,
    )


def local(
    intersection,
    density,
    hamiltonian,
    intersection_pattern,
    density_pattern,
    hamiltonian_pattern,
    product_filter,
):
    left_factor = mask_left(intersection, intersection_pattern)
    right_factor = mask_right(density, density_pattern)
    raw_product = multiply(left_factor, right_factor)
    filtered = mask_left(raw_product.astype(jnp.bfloat16), product_filter)
    masked_ham = mask_right(hamiltonian, hamiltonian_pattern)
    return multiply(filtered, masked_ham).astype(jnp.bfloat16)


def solution(mesh):
    placed = (
        P("row", "layer", "col"),
        P("layer", "row", None, "col"),
        P("layer", "row", None, "col"),
        P("row", "layer", "col"),
        P("layer", "row", None, "col"),
        P("layer", "row", None, "col"),
        P("row", "layer", "col"),
    )
    return jax.shard_map(
        local, mesh=mesh, in_specs=placed, out_specs=P("row", "layer", "col"), check_vma=False
    )
```

profile of v0, /device:TPU:0, one launch (start us, length us, event | category | flops | bytes accessed | tf_op | source)
XLA Modules:
  0.0 161.6 jit_solution(11556054652740069047)
XLA Ops:
  6.5 0.0 all-gather.7.cloned.1.call-start
  6.5 0.7 convert_bitcast_fusion.1
  7.2 0.2 mul.47
  7.4 0.0 copy-start.1
  7.4 0.1 mul.48
  7.6 0.8 copy-done.1
  8.4 0.0 copy-start.4
  8.4 0.8 mul.49
  9.2 0.0 copy-start
  9.2 0.0 all-gather.7.cloned.1.call-update
  9.2 0.0 all-gather.5.cloned.1.call-start
  9.3 0.0 copy-done.4
  9.3 0.1 copy.8
  9.4 0.2 mul.44
  9.6 0.5 copy-done
  10.2 0.7 bitcast_multiply_fusion.1
  10.9 0.0 all-gather.5.cloned.1.call-update
  10.9 0.0 reduce-scatter.3.cloned.1.call-start
  11.0 29.0 %all-gather.7.cloned.1.call-done = bf16[1024,512]{1,0:T(8,128)(2,1)} async-done(((bf16[256,512]{1,0:T(8,128)(2,1)}), bf16[1024,512]{1,0:T(8,128)(2,1)}) %all-gather.7.cloned.1.call-update) | async-done | bytes 1048592 | tf_op jit(solution)/shard_map/all_gather | solution.py:36
  40.0 17.9 %all-gather.5.cloned.1.call-done = bf16[512,1024]{1,0:T(8,128)(2,1)} async-done(((bf16[512,256]{1,0:T(8,128)(2,1)}), bf16[512,1024]{1,0:T(8,128)(2,1)}) %all-gather.5.cloned.1.call-update) | async-done | bytes 1048592 | tf_op jit(solution)/shard_map/all_gather | solution.py:30
  57.9 3.3 %fusion = f32[512,512]{0,1:T(8,128)} fusion(bf16[512,1024]{1,0:T(8,128)(2,1)} %all-gather.5.cloned.1.call-done, bf16[1024,512]{1,0:T(8,128)(2,1)} %all-gather.7.cloned.1.call-done), kind=kOutput, calls=%fused_computation.6 | convolution fusion | flops 536870912 | bytes 3145728 | tf_op jit(solution)/shard_map/dot_general | solution.py:34
  61.2 0.0 copy-start.3
  61.2 0.0 reduce-scatter.3.cloned.1.call-update
  61.2 0.0 all-gather.11.cloned.1.call-start
  61.3 0.6 copy-done.3
  61.9 0.2 mul.53
  62.1 0.0 copy-start.2
  62.1 0.1 mul.54
  62.2 0.8 copy-done.2
  63.1 0.8 mul.55
  63.9 0.0 copy-start.5
  63.9 0.0 all-gather.11.cloned.1.call-update
  63.9 0.0 all-gather.9.cloned.1.call-start
  64.0 0.6 copy-done.5
  64.6 17.1 %reduce-scatter.3.cloned.1.call-done = f32[512,1,256]{0,2,1:T(8,128)} async-done(((f32[512,2,256]{0,2,1:T(8,128)}), f32[512,1,256]{0,2,1:T(8,128)}) %reduce-scatter.3.cloned.1.call-update) | async-done | bytes 524304 | tf_op jit(solution)/shard_map/reduce_scatter | solution.py:39
  81.7 0.1 mul.50
  81.9 1.8 %bitcast_multiply_fusion = bf16[512,256]{0,1:T(8,128)(2,1)} fusion(bf16[32,8,4,128]{3,2,1,0:T(4,128)(2,1)S(1)} %bitcast.39, f32[512,1,256]{0,2,1:T(8,128)} %reduce-scatter.3.cloned.1.call-done), kind=kLoop, calls=%fused_computation | loop fusion | flops 262144 | bytes 1048576 | tf_op jit(solution)/shard_map/mul | solution.py:14
  83.7 0.0 all-gather.9.cloned.1.call-update
  83.7 0.0 reduce-scatter.5.cloned.1.call-start
  83.7 27.4 %all-gather.11.cloned.1.call-done = bf16[1024,512]{1,0:T(8,128)(2,1)} async-done(((bf16[256,512]{1,0:T(8,128)(2,1)}), bf16[1024,512]{1,0:T(8,128)(2,1)}) %all-gather.11.cloned.1.call-update) | async-done | bytes 1048592 | tf_op jit(solution)/shard_map/all_gather | solution.py:36
  111.2 17.7 %all-gather.9.cloned.1.call-done = bf16[512,1024]{0,1:T(8,128)(2,1)} async-done(((bf16[512,256]{0,1:T(8,128)(2,1)}), bf16[512,1024]{0,1:T(8,128)(2,1)}) %all-gather.9.cloned.1.call-update) | async-done | bytes 1048592 | tf_op jit(solution)/shard_map/all_gather | solution.py:30
  128.9 2.3 %fusion.1 = f32[512,512]{0,1:T(8,128)S(1)} fusion(bf16[512,1024]{0,1:T(8,128)(2,1)} %all-gather.9.cloned.1.call-done, bf16[1024,512]{1,0:T(8,128)(2,1)} %all-gather.11.cloned.1.call-done), kind=kOutput, calls=%fused_computation.7 | convolution fusion | flops 536870912 | bytes 3145728 | tf_op jit(solution)/shard_map/dot_general | solution.py:34
  131.2 1.3 copy.9
  132.5 0.0 reduce-scatter.5.cloned.1.call-update
  132.5 20.5 %reduce-scatter.5.cloned.1.call-done = f32[512,1,256]{2,0,1:T(8,128)} async-done(((f32[512,2,256]{2,0,1:T(8,128)}), f32[512,1,256]{2,0,1:T(8,128)}) %reduce-scatter.5.cloned.1.call-update) | async-done | bytes 524304 | tf_op jit(solution)/shard_map/reduce_scatter | solution.py:39
  153.0 1.8 %convert_element_type.59 = bf16[512,1,256]{2,0,1:T(8,128)(2,1)} convert(f32[512,1,256]{2,0,1:T(8,128)} %reduce-scatter.5.cloned.1.call-done) | non-fusion elementwise | flops 131072 | bytes 786432 | tf_op jit(solution)/shard_map/convert_element_type | solution.py:61
  (5 shorter events, 0.1 us)
Async XLA Ops:
  6.5 33.5 %all-gather.7.cloned.1.call-start = ((), (), s32[]{:S(2)}) async-start(), calls=%async_computation.3 | async-start | bytes 1310720 | tf_op jit(solution)/shard_map/all_gather | solution.py:36
  7.4 1.0 copy-start.1
  8.4 0.9 copy-start.4
  9.2 0.9 copy-start
  9.2 48.7 %all-gather.5.cloned.1.call-start = ((), (), s32[]{:S(2)}) async-start(), calls=%async_computation.2 | async-start | bytes 1310720 | tf_op jit(solution)/shard_map/all_gather | solution.py:30
  10.9 70.8 %reduce-scatter.3.cloned.1.call-start = ((), (), s32[]{:S(2)}) async-start(), calls=%async_computation.4 | async-start | bytes 1572864 | tf_op jit(solution)/shard_map/reduce_scatter | solution.py:39
  61.2 0.7 copy-start.3
  61.2 49.9 %all-gather.11.cloned.1.call-start = ((), (), s32[]{:S(2)}) async-start(), calls=%async_computation.6 | async-start | bytes 1310720 | tf_op jit(solution)/shard_map/all_gather | solution.py:36
  62.1 1.0 copy-start.2
  63.9 0.7 copy-start.5
  63.9 65.0 %all-gather.9.cloned.1.call-start = ((), (), s32[]{:S(2)}) async-start(), calls=%async_computation.5 | async-start | bytes 1310720 | tf_op jit(solution)/shard_map/all_gather | solution.py:30
  83.7 69.3 %reduce-scatter.5.cloned.1.call-start = ((), (), s32[]{:S(2)}) async-start(), calls=%async_computation.7 | async-start | bytes 1572864 | tf_op jit(solution)/shard_map/reduce_scatter | solution.py:39
Sparse Core Ops, SparseCore 0:
  9.4 30.6 all-gather.6
  41.6 16.3 all-gather.4
  61.4 20.3 reduce-scatter.2
  83.2 27.9 all-gather.10
  112.7 16.2 all-gather.8
  132.7 20.3 reduce-scatter.4
where the time goes:
time: 162 us
  waiting for transfers between devices  130 us (80%)
  between operations  13.6 us (8%)
  other arithmetic  6.58 us (4%)
  local copies, waits for them, and re-layouts  5.88 us (4%)
  matrix products  5.57 us (3%)
    all_gather x2, waiting for transfers between devices, multiply(): lax.all_gather(right_tile, 'row', axis=0, tiled=True)  56.5 us
    reduce_scatter x2, waiting for transfers between devices, multiply(): lax.psum_scatter(partial_value.reshape(row_count, layers, column_span), '...  37.6 us
    all_gather x2, waiting for transfers between devices, multiply(): whole_left = lax.all_gather(left_tile, 'col', axis=1, tiled=True)  35.6 us
    dot_general x2, matrix products, multiply(): jnp.dot(whole_left, lax.all_gather(right_tile, 'row', axis=0, tiled=True)...  5.57 us
    unnamed x14, local copies, waits for them, and re-layouts  3.49 us
  transfers between devices with their start and end apart: 6, of which 6 were waited for; matrix products, arithmetic and copies ran while one was open for 3% of the time, Pallas kernels for 0%

commit v1 on v0

v1 whole, which is shorter than its diff:
```python
import jax
import jax.numpy as jnp
from jax import lax
from jax.experimental import pallas as pl
from jax.experimental.pallas import tpu as pltpu
from jax.sharding import PartitionSpec as P

BLOCK = 128
CORES = 2
VMEM_BYTES = 48 * 1024 * 1024


def masked(value, flag):
    return value * flag.astype(jnp.float32).astype(value.dtype)


def mask_kernel(s_ref, p_ref, h_ref, s_pat, p_pat, h_pat, s_out, p_own, p_other, h_own, h_other):
    layer = lax.axis_index("layer")
    for i in range(s_pat.shape[0]):
        for j in range(s_pat.shape[2]):
            at = (pl.ds(i * BLOCK, BLOCK), pl.ds(j * BLOCK, BLOCK))
            s_out[at] = masked(s_ref[at[0], 0, at[1]], s_pat[i, 0, j])
    for full, pat, own, other in ((p_ref, p_pat, p_own, p_other), (h_ref, h_pat, h_own, h_other)):
        for out, half in ((own, layer), (other, 1 - layer)):
            for i in range(pat.shape[1]):
                for j in range(pat.shape[3]):
                    at = (pl.ds(i * BLOCK, BLOCK), pl.ds(j * BLOCK, BLOCK))
                    out[at] = masked(full[half, at[0], at[1]], pat[0, i, half, j])


def mask_all(s, p, h, s_pat, p_pat, h_pat):
    rows, _, cols = s.shape
    k_rows = p.shape[1]
    tile = jax.ShapeDtypeStruct((k_rows, cols), s.dtype)
    vmem = pl.BlockSpec(memory_space=pltpu.VMEM)
    smem = pl.BlockSpec(memory_space=pltpu.SMEM)
    return pl.pallas_call(
        mask_kernel,
        out_shape=(jax.ShapeDtypeStruct((rows, cols), s.dtype), tile, tile, tile, tile),
        in_specs=[vmem] * 3 + [smem] * 3,
        out_specs=(vmem,) * 5,
        compiler_params=pltpu.CompilerParams(vmem_limit_bytes=VMEM_BYTES),
        name="mask_all",
    )(s, p[0].transpose(1, 0, 2), h[0].transpose(1, 0, 2), s_pat, p_pat, h_pat)


def product(left, right, pattern, half):
    rows, cols = left[0][1].shape
    k_rows = right[0][1].shape[0]
    n_left, n_right = len(left), len(right)

    def kernel(*refs):
        left_refs = refs[:n_left]
        right_refs = refs[n_left : n_left + n_right]
        rest = refs[n_left + n_right :]
        out, whole = rest[-2], rest[-1]
        row, col, layer = (lax.axis_index(a) for a in ("row", "col", "layer"))
        for (masks, _), ref in zip(right, right_refs):
            at = (layer ^ masks[1]) * half + (row ^ masks[0]) * k_rows
            whole[pl.ds(pl.multiple_of(at, k_rows), k_rows), :] = ref[...]
        total = jnp.zeros((rows, cols), jnp.float32)
        for (masks, _), ref in zip(left, left_refs):
            at = (layer ^ masks[1]) * half + (col ^ masks[0]) * cols
            total += jnp.dot(
                ref[...], whole[pl.ds(pl.multiple_of(at, cols), cols), :], preferred_element_type=jnp.float32
            )
        total = total.astype(jnp.bfloat16)
        if pattern is None:
            out[:, 0, :] = total
        else:
            out[...] = total
            for i in range(pattern.shape[0]):
                for j in range(pattern.shape[2]):
                    at = (pl.ds(i * BLOCK, BLOCK), pl.ds(j * BLOCK, BLOCK))
                    out[at] = masked(out[at], rest[0][i, 0, j])

    vmem = pl.BlockSpec(memory_space=pltpu.VMEM)
    smem = pl.BlockSpec(memory_space=pltpu.SMEM)
    extra = [] if pattern is None else [pattern]
    out_shape = (rows, 1, cols) if pattern is None else (rows, cols)
    return pl.pallas_call(
        kernel,
        out_shape=jax.ShapeDtypeStruct(out_shape, jnp.bfloat16),
        in_specs=[vmem] * (n_left + n_right) + [smem] * len(extra),
        out_specs=vmem,
        scratch_shapes=[pltpu.VMEM((2 * half, cols), jnp.bfloat16)],
        compiler_params=pltpu.CompilerParams(vmem_limit_bytes=VMEM_BYTES),
        name="product",
    )(*[t for _, t in left], *[t for _, t in right], *extra)


def exchange(value, axes, mask):
    sizes = [lax.axis_size(a) for a in axes]
    if len(axes) == 1:
        return lax.ppermute(value, axes[0], [(i, i ^ mask[0]) for i in range(sizes[0])])
    pairs = [
        (i * sizes[1] + j, (i ^ mask[0]) * sizes[1] + (j ^ mask[1])) for i in range(sizes[0]) for j in range(sizes[1])
    ]
    return lax.ppermute(value, axes, pairs)


def along_row(tile):
    have = [(0, tile)]
    mask = lax.axis_size("row") - 1
    while mask:
        have += [(m ^ mask, exchange(t, ("row",), (mask,))) for m, t in have]
        mask >>= 1
    return have


def over_plane(tile):
    have = [((0, 0), tile)]
    n_col = lax.axis_size("col")
    for m_col in range(0, n_col, CORES):
        for m_layer in range(2):
            if m_col or m_layer:
                have.append(((m_col, m_layer), exchange(tile, ("col", "layer"), (m_col, m_layer))))
    return have + [((m[0] ^ 1, m[1]), exchange(t, ("col",), (1,))) for m, t in have]


def gather_right(own, other):
    other = exchange(other, ("layer",), (1,))
    return [((m, 0), t) for m, t in along_row(own)] + [((m, 1), t) for m, t in along_row(other)]


def local(s, p, h, s_pat, p_pat, h_pat, keep):
    half = p.shape[1] * lax.axis_size("row")
    left, p_own, p_other, h_own, h_other = mask_all(s, p, h, s_pat, p_pat, h_pat)
    filtered = product(over_plane(left), gather_right(p_own, p_other), keep, half)
    return product(over_plane(filtered), gather_right(h_own, h_other), None, half)


def solution(mesh):
    left = P("row", "layer", "col")
    right = P("layer", "row", None, "col")
    return jax.shard_map(
        local,
        mesh=mesh,
        in_specs=(left, right, right, left, right, right, left),
        out_specs=left,
        check_vma=False,
    )
```

time: 162 us -> 60.8 us (0.38)
  waiting for transfers between devices: 130 us -> 23.2 us
  starting transfers between devices: 0.21 us -> 30.1 us
  between operations: 13.6 us -> 0.11 us
  other arithmetic: 6.58 us -> 0 us
  matrix products: 5.57 us -> 0 us
  Pallas kernels: 0 us -> 4.06 us
  local copies, waits for them, and re-layouts: 5.88 us -> 3.11 us
    all_gather x4 -> x0, waiting for transfers between devices: 92.1 us -> none  [the longest x2 56.5 us: multiply(): lax.all_gather(right_tile, 'row', axis=0, tiled=True)]
    reduce_scatter x2 -> x0, waiting for transfers between devices: 37.6 us -> none  [multiply(): lax.psum_scatter(partial_value.reshape(row_count, layers, column_span), '...]
    ppermute x0 -> x28, starting transfers between devices: none -> 30.1 us  [the longest x22 23.1 us: exchange(): lax.ppermute(value, axes[0], [(i, i ^ mask[0]) for i in range(sizes[0])])]
    ppermute x0 -> x28, waiting for transfers between devices: none -> 23.2 us  [the longest x22 21.2 us: exchange(): lax.ppermute(value, axes[0], [(i, i ^ mask[0]) for i in range(sizes[0])])]
    dot_general x2 -> x0, matrix products: 5.57 us -> none  [multiply(): jnp.dot(whole_left, lax.all_gather(right_tile, 'row', axis=0, tiled=True)...]
    mul x4 -> x0, other arithmetic: 4.11 us -> none  [the longest x2 2.55 us: mask_left(): blocks * pattern.reshape(row_blocks, 1, col_blocks, 1).astype(jnp.bfloat16)]
    pallas_call x0 -> x3, Pallas kernels: none -> 4.06 us  [the longest x2 2.35 us: product(): pl.pallas_call(kernel, out_shape=jax.ShapeDtypeStruct(out_shape, jnp.bflo...]
    convert_element_type x5 -> x0, other arithmetic: 2.47 us -> none  [the longest x1 1.77 us: local(): return multiply(filtered, masked_ham).astype(jnp.bfloat16)]
  transfers between devices with their start and end apart: 6 -> 28, of which waited for: 6 -> 10; matrix products, arithmetic and copies ran while one was open for 3% -> 0% of each run, Pallas kernels for 0% -> 2%
where the time goes in v1:
time: 60.8 us; the launch traced here: 60.6 us
  starting transfers between devices  30.1 us (50%)
  waiting for transfers between devices  23.2 us (38%)
  Pallas kernels  4.06 us (7%)
  local copies, waits for them, and re-layouts  3.11 us (5%)
    ppermute x22, starting transfers between devices, exchange(): lax.ppermute(value, axes[0], [(i, i ^ mask[0]) for i in range(sizes[0])])  23.1 us
    ppermute x22, waiting for transfers between devices, exchange(): lax.ppermute(value, axes[0], [(i, i ^ mask[0]) for i in range(sizes[0])])  21.2 us
    ppermute x6, starting transfers between devices, exchange(): return lax.ppermute(value, axes, pairs)  7.04 us
    pallas_call x2, Pallas kernels, product(): pl.pallas_call(kernel, out_shape=jax.ShapeDtypeStruct(out_shape, jnp.bflo...  2.35 us
    unnamed x15, local copies, waits for them, and re-layouts  2.29 us
    ppermute x6, waiting for transfers between devices, exchange(): return lax.ppermute(value, axes, pairs)  1.99 us
    pallas_call x1, Pallas kernels, mask_all(): pl.pallas_call(mask_kernel, out_shape=(jax.ShapeDtypeStruct((rows, cols),...  1.7 us
  transfers between devices with their start and end apart: 28, of which 10 were waited for; matrix products, arithmetic and copies ran while one was open for 0% of the time, Pallas kernels for 2%

profile of v1, /device:TPU:0, one launch (start us, length us, event | category | flops | bytes accessed | tf_op | source)
XLA Modules:
  0.0 60.6 jit_solution(14030923889597607657)
XLA Ops:
  0.0 1.4 %copy.10.s_ref = bf16[512,1,256]{2,1,0:T(2,128)(2,1)S(1)} copy(bf16[512,1,256]{2,0,1:T(8,128)(2,1)} %param.7) | data formatting | bytes 524288 | tf_op args[0]
  1.4 0.1 copy.11.s_pat
  1.5 0.1 copy_bitcast_fusion
  1.6 0.0 copy-start
  1.6 0.6 copy-done.1
  2.2 0.1 copy-done
  2.3 1.7 %mask_all.1 = (bf16[512,256]{1,0:T(8,128)(2,1)S(1)}, bf16[256,256]{1,0:T(8,128)(2,1)S(1)}, bf16[256,256]{1,0:T(8,128)(2,1)S(1)}, bf16[256,256]{1,0:T(8,128)(2,1)S(1)}, bf16[256,256]{1,0:T(8,128)(2,1)S(1)}) custom-call(bf16[512,1,256]{2,1,0:T(2,128)(2,1)S(1)} %copy.10.s_ref, bf16[2,256,256]{2,1,0:T(8,128)(2,1)S(1)} %get-tuple-element.16.p_ref, ...), custom_call_target="tpu_custom_call" | custom-call | tf_op jit(solution)/shard_map/mask_all/pallas_call | solution.py:37
  4.0 3.0 %collective-permute-start.10 = (bf16[256,256]{1,0:T(8,128)(2,1)S(1)}, bf16[256,256]{1,0:T(8,128)(2,1)S(1)}, u32[]{:S(2)}, u32[]{:S(2)}) collective-permute-start(bf16[256,256]{1,0:T(8,128)(2,1)S(1)} %get-tuple-element.12), channel_id=1, source_target_pairs={{0,1},{1,0},{2,3},{3,2},{4,5},{5,4},{6,7},{7,6},{8,9},{9,8},{10,11... | collective-permute-start | bytes 393224 | tf_op jit(solution)/shard_map/ppermute | solution.py:95
  7.0 3.6 %collective-permute-start.7 = (bf16[256,256]{1,0:T(8,128)(2,1)S(1)}, bf16[256,256]{1,0:T(8,128)(2,1)S(1)}, u32[]{:S(2)}, u32[]{:S(2)}) collective-permute-start(bf16[256,256]{1,0:T(8,128)(2,1)S(1)} %get-tuple-element.11.refs_8_), channel_id=1, source_target_pairs={{0,24},{8,16},{16,8},{24,0},{1,25},{9,17},{17,9},{25,1},{2,26},{10... | collective-permute-start | bytes 393224 | tf_op jit(solution)/shard_map/ppermute | solution.py:95
  10.7 0.5 collective-permute-start
  11.2 1.5 %collective-permute-start.1 = (bf16[512,256]{1,0:T(8,128)(2,1)S(1)}, bf16[512,256]{1,0:T(8,128)(2,1)S(1)}, u32[]{:S(2)}, u32[]{:S(2)}) collective-permute-start(bf16[512,256]{1,0:T(8,128)(2,1)S(1)} %get-tuple-element.10.refs_0_), channel_id=1, source_target_pairs={{0,4},{1,5},{2,6},{3,7},{4,0},{5,1},{6,2},{7,3},{8,12},{9,13},{10,... | collective-permute-start | bytes 786440 | tf_op jit(solution)/shard_map/ppermute | solution.py:99
  12.7 1.5 %collective-permute-start.2 = (bf16[512,256]{1,0:T(8,128)(2,1)S(1)}, bf16[512,256]{1,0:T(8,128)(2,1)S(1)}, u32[]{:S(2)}, u32[]{:S(2)}) collective-permute-start(bf16[512,256]{1,0:T(8,128)(2,1)S(1)} %get-tuple-element.10.refs_0_), channel_id=1, source_target_pairs={{0,5},{1,4},{2,7},{3,6},{4,1},{5,0},{6,3},{7,2},{8,13},{9,12},{10,... | collective-permute-start | bytes 786440 | tf_op jit(solution)/shard_map/ppermute | solution.py:99
  14.1 0.0 collective-permute-done.10.refs_12_
  14.1 0.0 collective-permute-start.3
  14.1 0.0 collective-permute-done.7.refs_9_
  14.2 2.2 %collective-permute-start.8 = (bf16[256,256]{1,0:T(8,128)(2,1)S(1)}, bf16[256,256]{1,0:T(8,128)(2,1)S(1)}, u32[]{:S(2)}, u32[]{:S(2)}) collective-permute-start(bf16[256,256]{1,0:T(8,128)(2,1)S(1)} %get-tuple-element.11.refs_8_), channel_id=1, source_target_pairs={{0,8},{8,0},{16,24},{24,16},{1,9},{9,1},{17,25},{25,17},{2,10},{10... | collective-permute-start | bytes 393224 | tf_op jit(solution)/shard_map/ppermute | solution.py:95
  16.4 3.7 %collective-permute-done.8.refs_10_ = bf16[256,256]{1,0:T(8,128)(2,1)S(1)} collective-permute-done((bf16[256,256]{1,0:T(8,128)(2,1)S(1)}, bf16[256,256]{1,0:T(8,128)(2,1)S(1)}, u32[]{:S(2)}, u32[]{:S(2)}) %collective-permute-start.8) | collective-permute-done | bytes 131104 | tf_op jit(solution)/shard_map/ppermute | solution.py:95
  20.1 2.4 %collective-permute-start.11 = (bf16[256,256]{1,0:T(8,128)(2,1)S(1)}, bf16[256,256]{1,0:T(8,128)(2,1)S(1)}, u32[]{:S(2)}, u32[]{:S(2)}) collective-permute-start(bf16[256,256]{1,0:T(8,128)(2,1)S(1)} %collective-permute-done.10.refs_12_), channel_id=1, source_target_pairs={{0,24},{8,16},{16,8},{24,0},{1,25},{9,17},{17,9},{25,1},{2,26},{10... | collective-permute-start | bytes 393224 | tf_op jit(solution)/shard_map/ppermute | solution.py:95
  22.5 0.0 collective-permute-done.refs_1_
  22.5 0.5 collective-permute-start.9
  23.0 0.0 collective-permute-done.1.refs_2_
  23.0 0.0 collective-permute-start.4
  23.0 2.0 %collective-permute-done.2.refs_3_ = bf16[512,256]{1,0:T(8,128)(2,1)S(1)} collective-permute-done((bf16[512,256]{1,0:T(8,128)(2,1)S(1)}, bf16[512,256]{1,0:T(8,128)(2,1)S(1)}, u32[]{:S(2)}, u32[]{:S(2)}) %collective-permute-start.2) | collective-permute-done | bytes 262176 | tf_op jit(solution)/shard_map/ppermute | solution.py:99
  24.9 0.0 collective-permute-start.5
  24.9 0.0 collective-permute-done.3.refs_4_
  24.9 0.5 collective-permute-start.6
  25.5 2.8 %collective-permute-done.11.refs_13_ = bf16[256,256]{1,0:T(8,128)(2,1)S(1)} collective-permute-done((bf16[256,256]{1,0:T(8,128)(2,1)S(1)}, bf16[256,256]{1,0:T(8,128)(2,1)S(1)}, u32[]{:S(2)}, u32[]{:S(2)}) %collective-permute-start.11) | collective-permute-done | bytes 131104 | tf_op jit(solution)/shard_map/ppermute | solution.py:95
  28.3 0.3 collective-permute-start.12
  28.6 0.3 collective-permute-done.9.refs_11_
  28.8 1.5 %collective-permute-start.13 = (bf16[256,256]{1,0:T(8,128)(2,1)S(1)}, bf16[256,256]{1,0:T(8,128)(2,1)S(1)}, u32[]{:S(2)}, u32[]{:S(2)}) collective-permute-start(bf16[256,256]{1,0:T(8,128)(2,1)S(1)} %collective-permute-done.11.refs_13_), channel_id=1, source_target_pairs={{0,8},{8,0},{16,24},{24,16},{1,9},{9,1},{17,25},{25,17},{2,10},{10... | collective-permute-start | bytes 393224 | tf_op jit(solution)/shard_map/ppermute | solution.py:95
  30.3 2.9 %collective-permute-done.12.refs_14_ = bf16[256,256]{1,0:T(8,128)(2,1)S(1)} collective-permute-done((bf16[256,256]{1,0:T(8,128)(2,1)S(1)}, bf16[256,256]{1,0:T(8,128)(2,1)S(1)}, u32[]{:S(2)}, u32[]{:S(2)}) %collective-permute-start.12) | collective-permute-done | bytes 131104 | tf_op jit(solution)/shard_map/ppermute | solution.py:95
  33.2 0.6 collective-permute-start.24
  33.8 0.1 copy.12.refs_16_
  33.9 0.7 %collective-permute-done.13.refs_15_ = bf16[256,256]{1,0:T(8,128)(2,1)S(1)} collective-permute-done((bf16[256,256]{1,0:T(8,128)(2,1)S(1)}, bf16[256,256]{1,0:T(8,128)(2,1)S(1)}, u32[]{:S(2)}, u32[]{:S(2)}) %collective-permute-start.13) | collective-permute-done | bytes 131104 | tf_op jit(solution)/shard_map/ppermute | solution.py:95
  34.6 2.2 %collective-permute-start.21 = (bf16[256,256]{1,0:T(8,128)(2,1)S(1)}, bf16[256,256]{1,0:T(8,128)(2,1)S(1)}, u32[]{:S(2)}, u32[]{:S(2)}) collective-permute-start(bf16[256,256]{1,0:T(8,128)(2,1)S(1)} %get-tuple-element.13.refs_8_), channel_id=1, source_target_pairs={{0,24},{8,16},{16,8},{24,0},{1,25},{9,17},{17,9},{25,1},{2,26},{10... | collective-permute-start | bytes 393224 | tf_op jit(solution)/shard_map/ppermute | solution.py:95
  36.8 0.0 collective-permute-done.4.refs_5_
  36.8 0.0 collective-permute-start.22
  36.8 0.0 collective-permute-done.5.refs_6_
  36.8 0.0 collective-permute-done.6.refs_7_
  36.8 1.4 %product.2.refs_0_ = bf16[512,256]{1,0:T(8,128)(2,1)S(1)} custom-call(bf16[512,256]{1,0:T(8,128)(2,1)S(1)} %get-tuple-element.10.refs_0_, bf16[512,256]{1,0:T(8,128)(2,1)S(1)} %collective-permute-done.refs_1_, bf16[512,256]{1,0:T(8,128)(2,1)S(1)} %collective-permute-done.1.refs_2_, bf16[512,256]{1,0:T(8,128)(2,1)S(1)} %collective-permute-done.2.refs_3_, ...), custom_call_target="tpu_custom_call" | custom-call | tf_op jit(solution)/shard_map/product/pallas_call | solution.py:81
  38.2 1.8 %collective-permute-start.14 = (bf16[512,256]{1,0:T(8,128)(2,1)S(1)}, bf16[512,256]{1,0:T(8,128)(2,1)S(1)}, u32[]{:S(2)}, u32[]{:S(2)}) collective-permute-start(bf16[512,256]{1,0:T(8,128)(2,1)S(1)} %product.2.refs_0_), channel_id=1, source_target_pairs={{0,1},{1,0},{2,3},{3,2},{4,5},{5,4},{6,7},{7,6},{8,9},{9,8},{10,11... | collective-permute-start | bytes 786440 | tf_op jit(solution)/shard_map/ppermute | solution.py:99
  40.0 1.5 %collective-permute-start.15 = (bf16[512,256]{1,0:T(8,128)(2,1)S(1)}, bf16[512,256]{1,0:T(8,128)(2,1)S(1)}, u32[]{:S(2)}, u32[]{:S(2)}) collective-permute-start(bf16[512,256]{1,0:T(8,128)(2,1)S(1)} %product.2.refs_0_), channel_id=1, source_target_pairs={{0,4},{1,5},{2,6},{3,7},{4,0},{5,1},{6,2},{7,3},{8,12},{9,13},{10,... | collective-permute-start | bytes 786440 | tf_op jit(solution)/shard_map/ppermute | solution.py:99
  41.5 0.0 collective-permute-done.24.refs_12_
  41.5 0.3 collective-permute-start.16
  41.8 0.0 collective-permute-done.21.refs_9_
  41.8 1.9 %collective-permute-start.25 = (bf16[256,256]{1,0:T(8,128)(2,1)S(1)}, bf16[256,256]{1,0:T(8,128)(2,1)S(1)}, u32[]{:S(2)}, u32[]{:S(2)}) collective-permute-start(bf16[256,256]{1,0:T(8,128)(2,1)S(1)} %collective-permute-done.24.refs_12_), channel_id=1, source_target_pairs={{0,24},{8,16},{16,8},{24,0},{1,25},{9,17},{17,9},{25,1},{2,26},{10... | collective-permute-start | bytes 393224 | tf_op jit(solution)/shard_map/ppermute | solution.py:95
  43.7 0.0 collective-permute-done.22.refs_10_
  43.7 0.9 %collective-permute-start.23 = (bf16[256,256]{1,0:T(8,128)(2,1)S(1)}, bf16[256,256]{1,0:T(8,128)(2,1)S(1)}, u32[]{:S(2)}, u32[]{:S(2)}) collective-permute-start(bf16[256,256]{1,0:T(8,128)(2,1)S(1)} %collective-permute-done.21.refs_9_), channel_id=1, source_target_pairs={{0,8},{8,0},{16,24},{24,16},{1,9},{9,1},{17,25},{25,17},{2,10},{10... | collective-permute-start | bytes 393224 | tf_op jit(solution)/shard_map/ppermute | solution.py:95
  44.6 4.3 %collective-permute-done.25.refs_13_ = bf16[256,256]{1,0:T(8,128)(2,1)S(1)} collective-permute-done((bf16[256,256]{1,0:T(8,128)(2,1)S(1)}, bf16[256,256]{1,0:T(8,128)(2,1)S(1)}, u32[]{:S(2)}, u32[]{:S(2)}) %collective-permute-start.25) | collective-permute-done | bytes 131104 | tf_op jit(solution)/shard_map/ppermute | solution.py:95
  48.9 1.2 %collective-permute-start.26 = (bf16[256,256]{1,0:T(8,128)(2,1)S(1)}, bf16[256,256]{1,0:T(8,128)(2,1)S(1)}, u32[]{:S(2)}, u32[]{:S(2)}) collective-permute-start(bf16[256,256]{1,0:T(8,128)(2,1)S(1)} %collective-permute-done.24.refs_12_), channel_id=1, source_target_pairs={{0,8},{8,0},{16,24},{24,16},{1,9},{9,1},{17,25},{25,17},{2,10},{10... | collective-permute-start | bytes 393224 | tf_op jit(solution)/shard_map/ppermute | solution.py:95
  50.2 1.1 %collective-permute-done.23.refs_11_ = bf16[256,256]{1,0:T(8,128)(2,1)S(1)} collective-permute-done((bf16[256,256]{1,0:T(8,128)(2,1)S(1)}, bf16[256,256]{1,0:T(8,128)(2,1)S(1)}, u32[]{:S(2)}, u32[]{:S(2)}) %collective-permute-start.23) | collective-permute-done | bytes 131104 | tf_op jit(solution)/shard_map/ppermute | solution.py:95
  51.3 0.0 collective-permute-start.17
  51.3 0.0 collective-permute-done.14.refs_1_
  51.3 0.5 collective-permute-start.18
  51.8 0.0 collective-permute-done.15.refs_2_
  51.8 0.1 collective-permute-start.19
  51.9 0.0 collective-permute-done.16.refs_3_
  51.9 0.4 collective-permute-start.20
  52.3 1.6 %collective-permute-done.26.refs_14_ = bf16[256,256]{1,0:T(8,128)(2,1)S(1)} collective-permute-done((bf16[256,256]{1,0:T(8,128)(2,1)S(1)}, bf16[256,256]{1,0:T(8,128)(2,1)S(1)}, u32[]{:S(2)}, u32[]{:S(2)}) %collective-permute-start.26) | collective-permute-done | bytes 131104 | tf_op jit(solution)/shard_map/ppermute | solution.py:95
  53.9 1.2 %collective-permute-start.27 = (bf16[256,256]{1,0:T(8,128)(2,1)S(1)}, bf16[256,256]{1,0:T(8,128)(2,1)S(1)}, u32[]{:S(2)}, u32[]{:S(2)}) collective-permute-start(bf16[256,256]{1,0:T(8,128)(2,1)S(1)} %collective-permute-done.25.refs_13_), channel_id=1, source_target_pairs={{0,8},{8,0},{16,24},{24,16},{1,9},{9,1},{17,25},{25,17},{2,10},{10... | collective-permute-start | bytes 393224 | tf_op jit(solution)/shard_map/ppermute | solution.py:95
  55.1 3.7 %collective-permute-done.27.refs_15_ = bf16[256,256]{1,0:T(8,128)(2,1)S(1)} collective-permute-done((bf16[256,256]{1,0:T(8,128)(2,1)S(1)}, bf16[256,256]{1,0:T(8,128)(2,1)S(1)}, u32[]{:S(2)}, u32[]{:S(2)}) %collective-permute-start.27) | collective-permute-done | bytes 131104 | tf_op jit(solution)/shard_map/ppermute | solution.py:95
  58.9 0.0 collective-permute-done.20.refs_7_
  58.9 0.9 %product.3 = bf16[512,1,256]{2,1,0:T(2,128)(2,1)S(1)} custom-call(bf16[512,256]{1,0:T(8,128)(2,1)S(1)} %product.2.refs_0_, bf16[512,256]{1,0:T(8,128)(2,1)S(1)} %collective-permute-done.14.refs_1_, bf16[512,256]{1,0:T(8,128)(2,1)S(1)} %collective-permute-done.15.refs_2_, bf16[512,256]{1,0:T(8,128)(2,1)S(1)} %collective-permute-done.16.refs_3_, ...), custom_call_target="tpu_custom_call" | custom-call | tf_op jit(solution)/shard_map/product/pallas_call | solution.py:81
  59.8 0.7 %copy.13 = bf16[512,1,256]{2,0,1:T(8,128)(2,1)} copy(bf16[512,1,256]{2,1,0:T(2,128)(2,1)S(1)} %product.3) | data formatting | bytes 524288 | tf_op jit(solution)/shard_map/product/pallas_call | solution.py:81
  (12 shorter events, 0.0 us)
Async XLA Ops:
  0.0 1.4 %copy-start.4 = (s32[4,1,2]{0,2,1:T(2,128)S(1)}, s32[4,1,2]{0,2,1:T(2,128)}, u32[]{:S(2)}) copy-start(s32[4,1,2]{0,2,1:T(2,128)} %param.10) | copy-start | bytes 100
  0.0 1.5 %copy-start.3 = (bf16[1,256,2,256]{3,2,1,0:T(2,128)(2,1)S(1)}, bf16[1,256,2,256]{3,2,1,0:T(2,128)(2,1)}, u32[]{:S(2)}) copy-start(bf16[1,256,2,256]{3,2,1,0:T(2,128)(2,1)} %param.8) | copy-start | bytes 786436
  0.0 1.5 %copy-start.2 = (bf16[1,256,2,256]{3,2,1,0:T(2,128)(2,1)S(1)}, bf16[1,256,2,256]{3,2,1,0:T(2,128)(2,1)}, u32[]{:S(2)}) copy-start(bf16[1,256,2,256]{3,2,1,0:T(2,128)(2,1)} %param.9) | copy-start | bytes 786436
  1.5 0.7 %copy-start.1 = (s32[1,2,2,2]{3,2,1,0:T(2,128)S(1)}, s32[1,2,2,2]{3,2,1,0:T(2,128)}, u32[]{:S(2)}) copy-start(s32[1,2,2,2]{3,2,1,0:T(2,128)} %h_pat.1) | copy-start | bytes 100
  1.6 0.7 %copy-start = (s32[1,2,2,2]{3,2,1,0:T(2,128)S(1)}, s32[1,2,2,2]{3,2,1,0:T(2,128)}, u32[]{:S(2)}) copy-start(s32[1,2,2,2]{3,2,1,0:T(2,128)} %p_pat.1) | copy-start | bytes 100
  4.0 10.1 %collective-permute-start.10 = (bf16[256,256]{1,0:T(8,128)(2,1)S(1)}, bf16[256,256]{1,0:T(8,128)(2,1)S(1)}, u32[]{:S(2)}, u32[]{:S(2)}) collective-permute-start(bf16[256,256]{1,0:T(8,128)(2,1)S(1)} %get-tuple-element.12), channel_id=1, source_target_pairs={{0,1},{1,0},{2,3},{3,2},{4,5},{5,4},{6,7},{7,6},{8,9},{9,8},{10,11... | collective-permute-start | bytes 393224 | tf_op jit(solution)/shard_map/ppermute | solution.py:95
  7.0 7.1 %collective-permute-start.7 = (bf16[256,256]{1,0:T(8,128)(2,1)S(1)}, bf16[256,256]{1,0:T(8,128)(2,1)S(1)}, u32[]{:S(2)}, u32[]{:S(2)}) collective-permute-start(bf16[256,256]{1,0:T(8,128)(2,1)S(1)} %get-tuple-element.11.refs_8_), channel_id=1, source_target_pairs={{0,24},{8,16},{16,8},{24,0},{1,25},{9,17},{17,9},{25,1},{2,26},{10... | collective-permute-start | bytes 393224 | tf_op jit(solution)/shard_map/ppermute | solution.py:95
  10.7 23.2 %copy-start.5 = (s32[4,1,2]{0,2,1:T(2,128)S(1)}, s32[4,1,2]{0,2,1:T(2,128)}, u32[]{:S(2)}) copy-start(s32[4,1,2]{0,2,1:T(2,128)} %param.13) | copy-start | bytes 100
  10.7 11.8 %collective-permute-start = (bf16[512,256]{1,0:T(8,128)(2,1)S(1)}, bf16[512,256]{1,0:T(8,128)(2,1)S(1)}, u32[]{:S(2)}, u32[]{:S(2)}) collective-permute-start(bf16[512,256]{1,0:T(8,128)(2,1)S(1)} %get-tuple-element.10.refs_0_), channel_id=1, source_target_pairs={{0,1},{1,0},{2,3},{3,2},{4,5},{5,4},{6,7},{7,6},{8,9},{9,8},{10,11... | collective-permute-start | bytes 786440 | tf_op jit(solution)/shard_map/ppermute | solution.py:99
  11.2 11.8 %collective-permute-start.1 = (bf16[512,256]{1,0:T(8,128)(2,1)S(1)}, bf16[512,256]{1,0:T(8,128)(2,1)S(1)}, u32[]{:S(2)}, u32[]{:S(2)}) collective-permute-start(bf16[512,256]{1,0:T(8,128)(2,1)S(1)} %get-tuple-element.10.refs_0_), channel_id=1, source_target_pairs={{0,4},{1,5},{2,6},{3,7},{4,0},{5,1},{6,2},{7,3},{8,12},{9,13},{10,... | collective-permute-start | bytes 786440 | tf_op jit(solution)/shard_map/ppermute | solution.py:99
  12.7 12.3 %collective-permute-start.2 = (bf16[512,256]{1,0:T(8,128)(2,1)S(1)}, bf16[512,256]{1,0:T(8,128)(2,1)S(1)}, u32[]{:S(2)}, u32[]{:S(2)}) collective-permute-start(bf16[512,256]{1,0:T(8,128)(2,1)S(1)} %get-tuple-element.10.refs_0_), channel_id=1, source_target_pairs={{0,5},{1,4},{2,7},{3,6},{4,1},{5,0},{6,3},{7,2},{8,13},{9,12},{10,... | collective-permute-start | bytes 786440 | tf_op jit(solution)/shard_map/ppermute | solution.py:99
  14.1 10.8 %collective-permute-start.3 = (bf16[512,256]{1,0:T(8,128)(2,1)S(1)}, bf16[512,256]{1,0:T(8,128)(2,1)S(1)}, u32[]{:S(2)}, u32[]{:S(2)}) collective-permute-start(bf16[512,256]{1,0:T(8,128)(2,1)S(1)} %get-tuple-element.10.refs_0_), channel_id=1, source_target_pairs={{0,2},{2,0},{4,6},{6,4},{1,3},{3,1},{5,7},{7,5},{8,10},{10,8},{12,... | collective-permute-start | bytes 786440 | tf_op jit(solution)/shard_map/ppermute | solution.py:95
  14.2 5.9 %collective-permute-start.8 = (bf16[256,256]{1,0:T(8,128)(2,1)S(1)}, bf16[256,256]{1,0:T(8,128)(2,1)S(1)}, u32[]{:S(2)}, u32[]{:S(2)}) collective-permute-start(bf16[256,256]{1,0:T(8,128)(2,1)S(1)} %get-tuple-element.11.refs_8_), channel_id=1, source_target_pairs={{0,8},{8,0},{16,24},{24,16},{1,9},{9,1},{17,25},{25,17},{2,10},{10... | collective-permute-start | bytes 393224 | tf_op jit(solution)/shard_map/ppermute | solution.py:95
  20.1 8.2 %collective-permute-start.11 = (bf16[256,256]{1,0:T(8,128)(2,1)S(1)}, bf16[256,256]{1,0:T(8,128)(2,1)S(1)}, u32[]{:S(2)}, u32[]{:S(2)}) collective-permute-start(bf16[256,256]{1,0:T(8,128)(2,1)S(1)} %collective-permute-done.10.refs_12_), channel_id=1, source_target_pairs={{0,24},{8,16},{16,8},{24,0},{1,25},{9,17},{17,9},{25,1},{2,26},{10... | collective-permute-start | bytes 393224 | tf_op jit(solution)/shard_map/ppermute | solution.py:95
  22.5 6.4 %collective-permute-start.9 = (bf16[256,256]{1,0:T(8,128)(2,1)S(1)}, bf16[256,256]{1,0:T(8,128)(2,1)S(1)}, u32[]{:S(2)}, u32[]{:S(2)}) collective-permute-start(bf16[256,256]{1,0:T(8,128)(2,1)S(1)} %collective-permute-done.7.refs_9_), channel_id=1, source_target_pairs={{0,8},{8,0},{16,24},{24,16},{1,9},{9,1},{17,25},{25,17},{2,10},{10... | collective-permute-start | bytes 393224 | tf_op jit(solution)/shard_map/ppermute | solution.py:95
  23.0 13.8 %collective-permute-start.4 = (bf16[512,256]{1,0:T(8,128)(2,1)S(1)}, bf16[512,256]{1,0:T(8,128)(2,1)S(1)}, u32[]{:S(2)}, u32[]{:S(2)}) collective-permute-start(bf16[512,256]{1,0:T(8,128)(2,1)S(1)} %collective-permute-done.refs_1_), channel_id=1, source_target_pairs={{0,2},{2,0},{4,6},{6,4},{1,3},{3,1},{5,7},{7,5},{8,10},{10,8},{12,... | collective-permute-start | bytes 786440 | tf_op jit(solution)/shard_map/ppermute | solution.py:95
  24.9 11.9 %collective-permute-start.5 = (bf16[512,256]{1,0:T(8,128)(2,1)S(1)}, bf16[512,256]{1,0:T(8,128)(2,1)S(1)}, u32[]{:S(2)}, u32[]{:S(2)}) collective-permute-start(bf16[512,256]{1,0:T(8,128)(2,1)S(1)} %collective-permute-done.1.refs_2_), channel_id=1, source_target_pairs={{0,2},{2,0},{4,6},{6,4},{1,3},{3,1},{5,7},{7,5},{8,10},{10,8},{12,... | collective-permute-start | bytes 786440 | tf_op jit(solution)/shard_map/ppermute | solution.py:95
  24.9 11.9 %collective-permute-start.6 = (bf16[512,256]{1,0:T(8,128)(2,1)S(1)}, bf16[512,256]{1,0:T(8,128)(2,1)S(1)}, u32[]{:S(2)}, u32[]{:S(2)}) collective-permute-start(bf16[512,256]{1,0:T(8,128)(2,1)S(1)} %collective-permute-done.2.refs_3_), channel_id=1, source_target_pairs={{0,2},{2,0},{4,6},{6,4},{1,3},{3,1},{5,7},{7,5},{8,10},{10,8},{12,... | collective-permute-start | bytes 786440 | tf_op jit(solution)/shard_map/ppermute | solution.py:95
  28.3 5.0 %collective-permute-start.12 = (bf16[256,256]{1,0:T(8,128)(2,1)S(1)}, bf16[256,256]{1,0:T(8,128)(2,1)S(1)}, u32[]{:S(2)}, u32[]{:S(2)}) collective-permute-start(bf16[256,256]{1,0:T(8,128)(2,1)S(1)} %collective-permute-done.10.refs_12_), channel_id=1, source_target_pairs={{0,8},{8,0},{16,24},{24,16},{1,9},{9,1},{17,25},{25,17},{2,10},{10... | collective-permute-start | bytes 393224 | tf_op jit(solution)/shard_map/ppermute | solution.py:95
  28.8 5.8 %collective-permute-start.13 = (bf16[256,256]{1,0:T(8,128)(2,1)S(1)}, bf16[256,256]{1,0:T(8,128)(2,1)S(1)}, u32[]{:S(2)}, u32[]{:S(2)}) collective-permute-start(bf16[256,256]{1,0:T(8,128)(2,1)S(1)} %collective-permute-done.11.refs_13_), channel_id=1, source_target_pairs={{0,8},{8,0},{16,24},{24,16},{1,9},{9,1},{17,25},{25,17},{2,10},{10... | collective-permute-start | bytes 393224 | tf_op jit(solution)/shard_map/ppermute | solution.py:95
  33.2 8.3 %collective-permute-start.24 = (bf16[256,256]{1,0:T(8,128)(2,1)S(1)}, bf16[256,256]{1,0:T(8,128)(2,1)S(1)}, u32[]{:S(2)}, u32[]{:S(2)}) collective-permute-start(bf16[256,256]{1,0:T(8,128)(2,1)S(1)} %get-tuple-element.14), channel_id=1, source_target_pairs={{0,1},{1,0},{2,3},{3,2},{4,5},{5,4},{6,7},{7,6},{8,9},{9,8},{10,11... | collective-permute-start | bytes 393224 | tf_op jit(solution)/shard_map/ppermute | solution.py:95
  34.6 7.2 %collective-permute-start.21 = (bf16[256,256]{1,0:T(8,128)(2,1)S(1)}, bf16[256,256]{1,0:T(8,128)(2,1)S(1)}, u32[]{:S(2)}, u32[]{:S(2)}) collective-permute-start(bf16[256,256]{1,0:T(8,128)(2,1)S(1)} %get-tuple-element.13.refs_8_), channel_id=1, source_target_pairs={{0,24},{8,16},{16,8},{24,0},{1,25},{9,17},{17,9},{25,1},{2,26},{10... | collective-permute-start | bytes 393224 | tf_op jit(solution)/shard_map/ppermute | solution.py:95
  36.8 6.9 %collective-permute-start.22 = (bf16[256,256]{1,0:T(8,128)(2,1)S(1)}, bf16[256,256]{1,0:T(8,128)(2,1)S(1)}, u32[]{:S(2)}, u32[]{:S(2)}) collective-permute-start(bf16[256,256]{1,0:T(8,128)(2,1)S(1)} %get-tuple-element.13.refs_8_), channel_id=1, source_target_pairs={{0,8},{8,0},{16,24},{24,16},{1,9},{9,1},{17,25},{25,17},{2,10},{10... | collective-permute-start | bytes 393224 | tf_op jit(solution)/shard_map/ppermute | solution.py:95
  38.2 13.1 %collective-permute-start.14 = (bf16[512,256]{1,0:T(8,128)(2,1)S(1)}, bf16[512,256]{1,0:T(8,128)(2,1)S(1)}, u32[]{:S(2)}, u32[]{:S(2)}) collective-permute-start(bf16[512,256]{1,0:T(8,128)(2,1)S(1)} %product.2.refs_0_), channel_id=1, source_target_pairs={{0,1},{1,0},{2,3},{3,2},{4,5},{5,4},{6,7},{7,6},{8,9},{9,8},{10,11... | collective-permute-start | bytes 786440 | tf_op jit(solution)/shard_map/ppermute | solution.py:99
  40.0 11.8 %collective-permute-start.15 = (bf16[512,256]{1,0:T(8,128)(2,1)S(1)}, bf16[512,256]{1,0:T(8,128)(2,1)S(1)}, u32[]{:S(2)}, u32[]{:S(2)}) collective-permute-start(bf16[512,256]{1,0:T(8,128)(2,1)S(1)} %product.2.refs_0_), channel_id=1, source_target_pairs={{0,4},{1,5},{2,6},{3,7},{4,0},{5,1},{6,2},{7,3},{8,12},{9,13},{10,... | collective-permute-start | bytes 786440 | tf_op jit(solution)/shard_map/ppermute | solution.py:99
  41.5 10.3 %collective-permute-start.16 = (bf16[512,256]{1,0:T(8,128)(2,1)S(1)}, bf16[512,256]{1,0:T(8,128)(2,1)S(1)}, u32[]{:S(2)}, u32[]{:S(2)}) collective-permute-start(bf16[512,256]{1,0:T(8,128)(2,1)S(1)} %product.2.refs_0_), channel_id=1, source_target_pairs={{0,5},{1,4},{2,7},{3,6},{4,1},{5,0},{6,3},{7,2},{8,13},{9,12},{10,... | collective-permute-start | bytes 786440 | tf_op jit(solution)/shard_map/ppermute | solution.py:99
  41.8 7.1 %collective-permute-start.25 = (bf16[256,256]{1,0:T(8,128)(2,1)S(1)}, bf16[256,256]{1,0:T(8,128)(2,1)S(1)}, u32[]{:S(2)}, u32[]{:S(2)}) collective-permute-start(bf16[256,256]{1,0:T(8,128)(2,1)S(1)} %collective-permute-done.24.refs_12_), channel_id=1, source_target_pairs={{0,24},{8,16},{16,8},{24,0},{1,25},{9,17},{17,9},{25,1},{2,26},{10... | collective-permute-start | bytes 393224 | tf_op jit(solution)/shard_map/ppermute | solution.py:95
  43.7 7.6 %collective-permute-start.23 = (bf16[256,256]{1,0:T(8,128)(2,1)S(1)}, bf16[256,256]{1,0:T(8,128)(2,1)S(1)}, u32[]{:S(2)}, u32[]{:S(2)}) collective-permute-start(bf16[256,256]{1,0:T(8,128)(2,1)S(1)} %collective-permute-done.21.refs_9_), channel_id=1, source_target_pairs={{0,8},{8,0},{16,24},{24,16},{1,9},{9,1},{17,25},{25,17},{2,10},{10... | collective-permute-start | bytes 393224 | tf_op jit(solution)/shard_map/ppermute | solution.py:95
  48.9 5.0 %collective-permute-start.26 = (bf16[256,256]{1,0:T(8,128)(2,1)S(1)}, bf16[256,256]{1,0:T(8,128)(2,1)S(1)}, u32[]{:S(2)}, u32[]{:S(2)}) collective-permute-start(bf16[256,256]{1,0:T(8,128)(2,1)S(1)} %collective-permute-done.24.refs_12_), channel_id=1, source_target_pairs={{0,8},{8,0},{16,24},{24,16},{1,9},{9,1},{17,25},{25,17},{2,10},{10... | collective-permute-start | bytes 393224 | tf_op jit(solution)/shard_map/ppermute | solution.py:95
  51.3 7.6 %collective-permute-start.17 = (bf16[512,256]{1,0:T(8,128)(2,1)S(1)}, bf16[512,256]{1,0:T(8,128)(2,1)S(1)}, u32[]{:S(2)}, u32[]{:S(2)}) collective-permute-start(bf16[512,256]{1,0:T(8,128)(2,1)S(1)} %product.2.refs_0_), channel_id=1, source_target_pairs={{0,2},{2,0},{4,6},{6,4},{1,3},{3,1},{5,7},{7,5},{8,10},{10,8},{12,... | collective-permute-start | bytes 786440 | tf_op jit(solution)/shard_map/ppermute | solution.py:95
  51.3 7.6 %collective-permute-start.18 = (bf16[512,256]{1,0:T(8,128)(2,1)S(1)}, bf16[512,256]{1,0:T(8,128)(2,1)S(1)}, u32[]{:S(2)}, u32[]{:S(2)}) collective-permute-start(bf16[512,256]{1,0:T(8,128)(2,1)S(1)} %collective-permute-done.14.refs_1_), channel_id=1, source_target_pairs={{0,2},{2,0},{4,6},{6,4},{1,3},{3,1},{5,7},{7,5},{8,10},{10,8},{12,... | collective-permute-start | bytes 786440 | tf_op jit(solution)/shard_map/ppermute | solution.py:95
  51.8 7.1 %collective-permute-start.19 = (bf16[512,256]{1,0:T(8,128)(2,1)S(1)}, bf16[512,256]{1,0:T(8,128)(2,1)S(1)}, u32[]{:S(2)}, u32[]{:S(2)}) collective-permute-start(bf16[512,256]{1,0:T(8,128)(2,1)S(1)} %collective-permute-done.15.refs_2_), channel_id=1, source_target_pairs={{0,2},{2,0},{4,6},{6,4},{1,3},{3,1},{5,7},{7,5},{8,10},{10,8},{12,... | collective-permute-start | bytes 786440 | tf_op jit(solution)/shard_map/ppermute | solution.py:95
  51.9 7.0 %collective-permute-start.20 = (bf16[512,256]{1,0:T(8,128)(2,1)S(1)}, bf16[512,256]{1,0:T(8,128)(2,1)S(1)}, u32[]{:S(2)}, u32[]{:S(2)}) collective-permute-start(bf16[512,256]{1,0:T(8,128)(2,1)S(1)} %collective-permute-done.16.refs_3_), channel_id=1, source_target_pairs={{0,2},{2,0},{4,6},{6,4},{1,3},{3,1},{5,7},{7,5},{8,10},{10,8},{12,... | collective-permute-start | bytes 786440 | tf_op jit(solution)/shard_map/ppermute | solution.py:95
  53.9 5.0 %collective-permute-start.27 = (bf16[256,256]{1,0:T(8,128)(2,1)S(1)}, bf16[256,256]{1,0:T(8,128)(2,1)S(1)}, u32[]{:S(2)}, u32[]{:S(2)}) collective-permute-start(bf16[256,256]{1,0:T(8,128)(2,1)S(1)} %collective-permute-done.25.refs_13_), channel_id=1, source_target_pairs={{0,8},{8,0},{16,24},{24,16},{1,9},{9,1},{17,25},{25,17},{2,10},{10... | collective-permute-start | bytes 393224 | tf_op jit(solution)/shard_map/ppermute | solution.py:95

commit v2 on v1

v2 whole, which is shorter than its diff:
```python
import jax
import jax.numpy as jnp
from jax import lax
from jax.experimental import pallas as pl
from jax.experimental.pallas import tpu as pltpu
from jax.sharding import PartitionSpec as P

BLOCK = 128
CORES = 2
VMEM_BYTES = 48 * 1024 * 1024


def masked(value, flag):
    return value * flag.astype(jnp.float32).astype(value.dtype)


def blocks(rows, cols):
    return [
        (i, j, (pl.ds(i * BLOCK, BLOCK), pl.ds(j * BLOCK, BLOCK))) for i in range(rows) for j in range(cols)
    ]


def mask_kernel(s_ref, p_ref, h_ref, s_pat, p_pat, h_pat, s_out, p_own, h_own, others):
    layer = lax.axis_index("layer")
    k_rows, cols = p_own.shape
    for full, pat, own, first in ((p_ref, p_pat, p_own, 0), (h_ref, h_pat, h_own, k_rows)):
        for i, j, at in blocks(pat.shape[1], pat.shape[3]):
            own[at] = masked(full[layer, at[0], at[1]], pat[0, i, layer, j])
            there = (pl.ds(first + i * BLOCK, BLOCK), at[1])
            others[there] = masked(full[1 - layer, at[0], at[1]], pat[0, i, 1 - layer, j])
    for i, j, at in blocks(s_pat.shape[1], s_pat.shape[0]):
        s_out[at] = masked(s_ref[at], s_pat[j, i])


def flat_pattern(pattern):
    return pattern.transpose(1, 2, 0).reshape(pattern.shape[2], pattern.shape[0])


def mask_all(s, p, h, s_pat, p_pat, h_pat):
    rows, _, cols = s.shape
    k_rows = p.shape[1]
    shapes = ((rows, cols), (k_rows, cols), (k_rows, cols), (2 * k_rows, cols))
    smem = pl.BlockSpec(memory_space=pltpu.SMEM)

    def whole(shape):
        return pl.BlockSpec(shape, lambda i: (0,) * len(shape))

    return pl.pallas_call(
        mask_kernel,
        grid=(1,),
        out_shape=tuple(jax.ShapeDtypeStruct(shape, s.dtype) for shape in shapes),
        in_specs=[whole((rows, cols)), whole((2, k_rows, cols)), whole((2, k_rows, cols))] + [smem] * 3,
        out_specs=tuple(whole(shape) for shape in shapes),
        compiler_params=pltpu.CompilerParams(vmem_limit_bytes=VMEM_BYTES),
        name="mask_all",
    )(s.reshape(rows, cols), p[0].transpose(1, 0, 2), h[0].transpose(1, 0, 2), flat_pattern(s_pat), p_pat, h_pat)


def product(left, right, keep, half):
    rows, cols = left[0][1].shape
    n_left, n_right = len(left), len(right)

    def kernel(*refs):
        left_refs = refs[:n_left]
        right_refs = refs[n_left : n_left + n_right]
        rest = refs[n_left + n_right :]
        out, whole = rest[-2], rest[-1]
        row, col, layer = (lax.axis_index(a) for a in ("row", "col", "layer"))
        k_rows = half // lax.axis_size("row")
        for (mask, layers, _), ref in zip(right, right_refs):
            for n, m in enumerate(layers):
                at = (layer ^ m) * half + (row ^ mask) * k_rows
                whole[pl.ds(pl.multiple_of(at, k_rows), k_rows), :] = ref[pl.ds(n * k_rows, k_rows), :]
        total = jnp.zeros((rows, cols), jnp.float32)
        for (masks, _), ref in zip(left, left_refs):
            at = (layer ^ masks[1]) * half + (col ^ masks[0]) * cols
            total += jnp.dot(
                ref[...], whole[pl.ds(pl.multiple_of(at, cols), cols), :], preferred_element_type=jnp.float32
            )
        out[...] = total.astype(jnp.bfloat16)
        if keep is not None:
            for i, j, at in blocks(keep.shape[1], keep.shape[0]):
                out[at] = masked(out[at], rest[0][j, i])

    vmem = pl.BlockSpec(memory_space=pltpu.VMEM)
    extra = [] if keep is None else [keep]
    return pl.pallas_call(
        kernel,
        out_shape=jax.ShapeDtypeStruct((rows, cols), jnp.bfloat16),
        in_specs=[vmem] * (n_left + n_right) + [pl.BlockSpec(memory_space=pltpu.SMEM)] * len(extra),
        out_specs=vmem,
        scratch_shapes=[pltpu.VMEM((2 * half, cols), jnp.bfloat16)],
        compiler_params=pltpu.CompilerParams(vmem_limit_bytes=VMEM_BYTES),
        name="product",
    )(*[t for _, t in left], *[t for *_, t in right], *extra)


def exchange(value, axes, mask):
    sizes = [lax.axis_size(a) for a in axes]
    if len(axes) == 1:
        return lax.ppermute(value, axes[0], [(i, i ^ mask[0]) for i in range(sizes[0])])
    pairs = [
        (i * sizes[1] + j, (i ^ mask[0]) * sizes[1] + (j ^ mask[1])) for i in range(sizes[0]) for j in range(sizes[1])
    ]
    return lax.ppermute(value, axes, pairs)


def after(value, *others):
    return lax.optimization_barrier((value, *others))[0] if others else value


WAITS = {
    "s20": ("p1",),
    "sc00": ("ph",),
    "sc01": ("p2", "q2", "q1", "ph",),
    "sc20": ("p2", "q2", "ph",),
    "sc21": ("p2", "q2",),
    "q2": ("ph",),
    "s01": ("q1",),
}
ORDER = (
    "ph", "p3", "sc00", "p1", "q1", "s21", "q3", "s01", "s20", "p2", "q2", "h3", "h1", "sc01", "sc20",
    "sc21", "x", "x21", "x01", "x20", "h2", "xc00", "xc01", "xc20", "xc21",
)


class Exchanges:
    def __init__(self):
        self.done = {}

    def add(self, name, value, axes, mask):
        gates = [self.done[n] for n in WAITS.get(name, ()) if n in self.done]
        self.done[name] = exchange(after(value, *gates), axes, mask)


def row_steps():
    have, steps, distance = [0], [], lax.axis_size("row") - 1
    while distance:
        new = [(m ^ distance, m, distance) for m in have]
        steps += new
        have += [m for m, _, _ in new]
        distance >>= 1
    return steps


def local(s, p, h, s_pat, p_pat, h_pat, keep):
    k = p.shape[1]
    half = k * lax.axis_size("row")
    s0, p0, h0, ph0 = mask_all(s, p, h, s_pat, p_pat, h_pat)
    ex = Exchanges()
    done = ex.done
    plane = [(c, l) for c in range(0, lax.axis_size("col"), CORES) for l in range(2)][1:]
    whole = {}

    def h2():
        if not whole:
            whole[0] = jnp.concatenate([h0, done["ph"][k:]], axis=0)
        return whole[0]

    def step(kind, mask, source, distance):
        if kind == "p":
            return lambda: ex.add(f"p{mask}", done[f"p{source}"] if source else p0, ("row",), (distance,))
        if kind == "h":
            return lambda: ex.add(f"h{mask}", done[f"h{source}"] if source else h2(), ("row",), (distance,))
        if source:
            return lambda: ex.add(f"q{mask}", done[f"q{source}"], ("row",), (distance,))
        return lambda: ex.add(f"q{mask}", ph0[:k], ("row", "layer"), (distance, 1))

    def tiles(kind, own):
        return {(0, 0): own, **{m: done[f"{kind}{m[0]}{m[1]}"] for m in plane}}

    def between(kind, own, m):
        return lambda: ex.add(f"{kind}{m[0]}{m[1]}", own(), ("col", "layer"), m)

    def cores(kind, own, m):
        return lambda: ex.add(f"{kind}c{m[0]}{m[1]}", tiles(kind, own())[m] if m != (0, 0) else own(), ("col",), (1,))

    sends = {"ph": lambda: ex.add("ph", ph0, ("layer",), (1,))}
    for mask, source, distance in row_steps():
        for kind in "pqh":
            sends[f"{kind}{mask}"] = step(kind, mask, source, distance)
    def factor(kind, own):
        mine = tiles(kind, own)
        return list(mine.items()) + [((m[0] ^ 1, m[1]), done[f"{kind}c{m[0]}{m[1]}"]) for m in mine]

    masks = [mask for mask, _, _ in row_steps()]

    def first():
        right = [(0, (0,), p0), (0, (1,), done["ph"])]
        right += [(m, (n,), done[f"{kind}{m}"]) for n, kind in enumerate("pq") for m in masks]
        gates = [done[n] for n in WAITS.get("x", ()) if n in done]
        done["x"] = product(factor("s", after(s0, *gates)), right, flat_pattern(keep), half)

    for kind, own in (("s", lambda: s0), ("x", lambda: done["x"])):
        if kind == "x":
            sends["x"] = first
        for m in plane:
            sends[f"{kind}{m[0]}{m[1]}"] = between(kind, own, m)
        for m in [(0, 0)] + plane:
            sends[f"{kind}c{m[0]}{m[1]}"] = cores(kind, own, m)
    for name in ORDER if set(ORDER) == set(sends) else list(sends):
        sends[name]()
    right = [(0, (0, 1), h2())] + [(m, (0, 1), done[f"h{m}"]) for m in masks]
    return product(factor("x", done["x"]), right, None, half).reshape(s.shape)


def solution(mesh):
    left = P("row", "layer", "col")
    right = P("layer", "row", None, "col")
    return jax.shard_map(
        local,
        mesh=mesh,
        in_specs=(left, right, right, left, right, right, left),
        out_specs=left,
        check_vma=False,
    )
```

time: 60.8 us -> 53.6 us (0.88)
  waiting for transfers between devices: 23.2 us -> 20.1 us
  starting transfers between devices: 30.1 us -> 27.7 us
  local copies, waits for them, and re-layouts: 3.11 us -> 1.85 us
    ppermute x22 -> x16, waiting for transfers between devices: 21.2 us -> 10.7 us  [exchange(): lax.ppermute(value, axes[0], [(i, i ^ mask[0]) for i in range(sizes[0])])]
    ppermute x22 -> x16, starting transfers between devices: 23.1 us -> 14.6 us  [exchange(): lax.ppermute(value, axes[0], [(i, i ^ mask[0]) for i in range(sizes[0])])]
    ppermute x6 -> x8, waiting for transfers between devices: 1.99 us -> 9.42 us  [exchange(): return lax.ppermute(value, axes, pairs)]
    ppermute x6 -> x8, starting transfers between devices: 7.04 us -> 13 us  [exchange(): return lax.ppermute(value, axes, pairs)]
    unnamed x15 -> x10, local copies, waits for them, and re-layouts: 2.29 us -> 0.69 us
    transpose x1, local copies, waits for them, and re-layouts: 0.07 us -> 1.14 us  [mask_all(): h[0].transpose(1, 0, 2)]
    pallas_call x1 -> x0, local copies, waits for them, and re-layouts: 0.74 us -> none  [product(): pl.pallas_call(kernel, out_shape=jax.ShapeDtypeStruct(out_shape, jnp.bflo...]
  transfers between devices with their start and end apart: 28 -> 24, of which waited for: 10 -> 9; matrix products, arithmetic and copies ran while one was open for 0% -> 0% of each run, Pallas kernels for 2% -> 3%
where the time goes in v2:
time: 53.6 us; the launch traced here: 53.5 us
  starting transfers between devices  27.7 us (52%)
  waiting for transfers between devices  20.1 us (38%)
  Pallas kernels  3.69 us (7%)
  local copies, waits for them, and re-layouts  1.85 us (3%)
    ppermute x16, starting transfers between devices, exchange(): lax.ppermute(value, axes[0], [(i, i ^ mask[0]) for i in range(sizes[0])])  14.6 us
    ppermute x8, starting transfers between devices, exchange(): return lax.ppermute(value, axes, pairs)  13 us
    ppermute x16, waiting for transfers between devices, exchange(): lax.ppermute(value, axes[0], [(i, i ^ mask[0]) for i in range(sizes[0])])  10.7 us
    ppermute x8, waiting for transfers between devices, exchange(): return lax.ppermute(value, axes, pairs)  9.42 us
    pallas_call x2, Pallas kernels, product(): pl.pallas_call(kernel, out_shape=jax.ShapeDtypeStruct((rows, cols), jnp.b...  2.91 us
    transpose x1, local copies, waits for them, and re-layouts, mask_all(): h[0].transpose(1, 0, 2)  1.14 us
  transfers between devices with their start and end apart: 24, of which 9 were waited for; matrix products, arithmetic and copies ran while one was open for 0% of the time, Pallas kernels for 3%

profile of v2, /device:TPU:0, one launch (start us, length us, event | category | flops | bytes accessed | tf_op | source)
XLA Modules:
  0.0 53.5 jit_solution(6617957773882813902)
XLA Ops:
  0.0 0.0 copy-start
  0.0 1.1 %copy_bitcast_fusion = (bf16[2,256,256]{2,1,0:T(8,128)(2,1)S(1)}, bf16[2,256,256]{2,1,0:T(8,128)(2,1)S(1)}) fusion(bf16[1,256,2,256]{3,2,1,0:T(2,128)(2,1)} %param.9, bf16[1,256,2,256]{3,2,1,0:T(2,128)(2,1)} %param.8), kind=kLoop, calls=%fused_computation.1 | loop fusion | bytes 1048576 | tf_op jit(solution)/shard_map/transpose | solution.py:56
  1.1 0.0 copy-start.2
  1.2 0.0 copy-start.1
  1.2 0.0 copy-start.3
  1.2 0.0 copy-done
  1.2 0.6 %copy-done.2 = s32[1,2,2,2]{3,2,1,0:T(2,128)S(1)} copy-done((s32[1,2,2,2]{3,2,1,0:T(2,128)S(1)}, s32[1,2,2,2]{3,2,1,0:T(2,128)}, u32[]{:S(2)}) %copy-start.2) | copy-done | bytes 56
  1.8 0.0 copy-done.1
  1.9 0.0 copy-done.3
  1.9 0.8 %mask_all.1 = (bf16[512,256]{1,0:T(8,128)(2,1)S(1)}, bf16[256,256]{1,0:T(8,128)(2,1)S(1)}, bf16[256,256]{1,0:T(8,128)(2,1)S(1)}, bf16[512,256]{1,0:T(8,128)(2,1)S(1)}) custom-call(bf16[512,256]{1,0:T(8,128)(2,1)S(1)} %bitcast.16, bf16[2,256,256]{2,1,0:T(8,128)(2,1)S(1)} %get-tuple-element.28.p_ref, bf16[2,256,256]{2,1,0:T(8,128)(2,1)S(1)} %get-tuple-element.27.h_ref, ...), custom_call_target="tpu_custom_call" | custom-call | tf_op jit(solution)/shard_map/mask_all/pallas_call | solution.py:48
  2.6 3.0 %collective-permute-start.5 = (bf16[512,256]{1,0:T(8,128)(2,1)S(1)}, bf16[512,256]{1,0:T(8,128)(2,1)S(1)}, u32[]{:S(2)}, u32[]{:S(2)}) collective-permute-start(bf16[512,256]{1,0:T(8,128)(2,1)S(1)} %get-tuple-element.17), channel_id=1, source_target_pairs={{0,1},{1,0},{2,3},{3,2},{4,5},{5,4},{6,7},{7,6},{8,9},{9,8},{10,11... | collective-permute-start | bytes 786440 | tf_op jit(solution)/shard_map/ppermute | solution.py:101
  5.7 1.6 %collective-permute-start = (bf16[256,256]{1,0:T(8,128)(2,1)S(1)}, bf16[256,256]{1,0:T(8,128)(2,1)S(1)}, u32[]{:S(2)}, u32[]{:S(2)}) collective-permute-start(bf16[256,256]{1,0:T(8,128)(2,1)S(1)} %slice.7), channel_id=1, source_target_pairs={{0,9},{1,8},{8,1},{9,0},{16,25},{17,24},{24,17},{25,16},{2,11},{3,... | collective-permute-start | bytes 393224 | tf_op jit(solution)/shard_map/ppermute | solution.py:105
  7.3 0.1 collective-permute-start.2
  7.4 4.9 %collective-permute-start.9 = (bf16[256,256]{1,0:T(8,128)(2,1)S(1)}, bf16[256,256]{1,0:T(8,128)(2,1)S(1)}, u32[]{:S(2)}, u32[]{:S(2)}) collective-permute-start(bf16[256,256]{1,0:T(8,128)(2,1)S(1)} %slice.7), channel_id=1, source_target_pairs={{0,25},{1,24},{8,17},{9,16},{16,9},{17,8},{24,1},{25,0},{2,27},{3,... | collective-permute-start | bytes 393224 | tf_op jit(solution)/shard_map/ppermute | solution.py:105
  12.3 0.2 collective-permute-start.7
  12.5 0.6 %collective-permute-done.refs_14_ = bf16[256,256]{1,0:T(8,128)(2,1)S(1)} collective-permute-done((bf16[256,256]{1,0:T(8,128)(2,1)S(1)}, bf16[256,256]{1,0:T(8,128)(2,1)S(1)}, u32[]{:S(2)}, u32[]{:S(2)}) %collective-permute-start) | collective-permute-done | bytes 131104 | tf_op jit(solution)/shard_map/ppermute | solution.py:105
  13.1 0.1 collective-permute-start.1
  13.2 0.6 %collective-permute-done.2.refs_11_ = bf16[256,256]{1,0:T(8,128)(2,1)S(1)} collective-permute-done((bf16[256,256]{1,0:T(8,128)(2,1)S(1)}, bf16[256,256]{1,0:T(8,128)(2,1)S(1)}, u32[]{:S(2)}, u32[]{:S(2)}) %collective-permute-start.2) | collective-permute-done | bytes 131104 | tf_op jit(solution)/shard_map/ppermute | solution.py:101
  13.8 1.5 %collective-permute-start.3 = (bf16[512,256]{1,0:T(8,128)(2,1)S(1)}, bf16[512,256]{1,0:T(8,128)(2,1)S(1)}, u32[]{:S(2)}, u32[]{:S(2)}) collective-permute-start(bf16[512,256]{1,0:T(8,128)(2,1)S(1)} %get-tuple-element.21.refs_0_), channel_id=1, source_target_pairs={{0,4},{1,5},{2,6},{3,7},{4,0},{5,1},{6,2},{7,3},{8,12},{9,13},{10,... | collective-permute-start | bytes 786440 | tf_op jit(solution)/shard_map/ppermute | solution.py:105
  15.2 5.7 %collective-permute-done.9.refs_13_ = bf16[256,256]{1,0:T(8,128)(2,1)S(1)} collective-permute-done((bf16[256,256]{1,0:T(8,128)(2,1)S(1)}, bf16[256,256]{1,0:T(8,128)(2,1)S(1)}, u32[]{:S(2)}, u32[]{:S(2)}) %collective-permute-start.9) | collective-permute-done | bytes 131104 | tf_op jit(solution)/shard_map/ppermute | solution.py:105
  20.9 1.4 %collective-permute-start.4 = (bf16[512,256]{1,0:T(8,128)(2,1)S(1)}, bf16[512,256]{1,0:T(8,128)(2,1)S(1)}, u32[]{:S(2)}, u32[]{:S(2)}) collective-permute-start(bf16[512,256]{1,0:T(8,128)(2,1)S(1)} %get-tuple-element.21.refs_0_), channel_id=1, source_target_pairs={{0,5},{1,4},{2,7},{3,6},{4,1},{5,0},{6,3},{7,2},{8,13},{9,12},{10,... | collective-permute-start | bytes 786440 | tf_op jit(solution)/shard_map/ppermute | solution.py:105
  22.3 0.0 collective-permute-done.7.refs_10_
  22.3 1.9 %collective-permute-start.8 = (bf16[256,256]{1,0:T(8,128)(2,1)S(1)}, bf16[256,256]{1,0:T(8,128)(2,1)S(1)}, u32[]{:S(2)}, u32[]{:S(2)}) collective-permute-start(bf16[256,256]{1,0:T(8,128)(2,1)S(1)} %collective-permute-done.7.refs_10_), channel_id=1, source_target_pairs={{0,8},{8,0},{16,24},{24,16},{1,9},{9,1},{17,25},{25,17},{2,10},{10... | collective-permute-start | bytes 393224 | tf_op jit(solution)/shard_map/ppermute | solution.py:101
  24.3 0.0 collective-permute-done.5.refs_9_
  24.3 0.1 collective-permute-start.10
  24.4 2.9 %collective-permute-done.8.refs_12_ = bf16[256,256]{1,0:T(8,128)(2,1)S(1)} collective-permute-done((bf16[256,256]{1,0:T(8,128)(2,1)S(1)}, bf16[256,256]{1,0:T(8,128)(2,1)S(1)}, u32[]{:S(2)}, u32[]{:S(2)}) %collective-permute-start.8) | collective-permute-done | bytes 131104 | tf_op jit(solution)/shard_map/ppermute | solution.py:101
  27.3 0.0 collective-permute-start.6
  27.3 1.9 %collective-permute-done.10.refs_15_ = bf16[256,256]{1,0:T(8,128)(2,1)S(1)} collective-permute-done((bf16[256,256]{1,0:T(8,128)(2,1)S(1)}, bf16[256,256]{1,0:T(8,128)(2,1)S(1)}, u32[]{:S(2)}, u32[]{:S(2)}) %collective-permute-start.10) | collective-permute-done | bytes 131104 | tf_op jit(solution)/shard_map/ppermute | solution.py:101
  29.2 0.0 collective-permute-done.1.refs_1_
  29.3 0.0 collective-permute-start.11
  29.3 0.0 collective-permute-done.3.refs_2_
  29.3 0.5 collective-permute-start.12
  29.8 0.0 collective-permute-done.4.refs_3_
  29.8 0.1 collective-permute-start.13
  29.9 0.0 copy-start.4
  29.9 3.1 %collective-permute-start.21 = (bf16[512,256]{1,0:T(8,128)(2,1)S(1)}, bf16[512,256]{1,0:T(8,128)(2,1)S(1)}, u32[]{:S(2)}, u32[]{:S(2)}) collective-permute-start(bf16[512,256]{1,0:T(8,128)(2,1)S(1)} %pad_maximum_fusion.refs_8_), channel_id=1, source_target_pairs={{0,24},{8,16},{16,8},{24,0},{1,25},{9,17},{17,9},{25,1},{2,26},{10... | collective-permute-start | bytes 786440 | tf_op jit(solution)/shard_map/ppermute | solution.py:101
  33.0 0.0 collective-permute-done.6.refs_4_
  33.0 0.2 collective-permute-start.22
  33.2 0.0 collective-permute-done.11.refs_5_
  33.2 0.0 collective-permute-done.12.refs_6_
  33.2 0.0 collective-permute-done.13.refs_7_
  33.2 0.0 copy-done.4
  33.2 1.4 %product.2.refs_0_ = bf16[512,256]{1,0:T(8,128)(2,1)S(1)} custom-call(bf16[512,256]{1,0:T(8,128)(2,1)S(1)} %get-tuple-element.21.refs_0_, bf16[512,256]{1,0:T(8,128)(2,1)S(1)} %collective-permute-done.1.refs_1_, bf16[512,256]{1,0:T(8,128)(2,1)S(1)} %collective-permute-done.3.refs_2_, bf16[512,256]{1,0:T(8,128)(2,1)S(1)} %collective-permute-done.4.refs_3_, ...), custom_call_target="tpu_custom_call" | custom-call | tf_op jit(solution)/shard_map/product/pallas_call | solution.py:87
  34.6 1.8 %collective-permute-start.14 = (bf16[512,256]{1,0:T(8,128)(2,1)S(1)}, bf16[512,256]{1,0:T(8,128)(2,1)S(1)}, u32[]{:S(2)}, u32[]{:S(2)}) collective-permute-start(bf16[512,256]{1,0:T(8,128)(2,1)S(1)} %product.2.refs_0_), channel_id=1, source_target_pairs={{0,1},{1,0},{2,3},{3,2},{4,5},{5,4},{6,7},{7,6},{8,9},{9,8},{10,11... | collective-permute-start | bytes 786440 | tf_op jit(solution)/shard_map/ppermute | solution.py:105
  36.4 1.5 %collective-permute-start.15 = (bf16[512,256]{1,0:T(8,128)(2,1)S(1)}, bf16[512,256]{1,0:T(8,128)(2,1)S(1)}, u32[]{:S(2)}, u32[]{:S(2)}) collective-permute-start(bf16[512,256]{1,0:T(8,128)(2,1)S(1)} %product.2.refs_0_), channel_id=1, source_target_pairs={{0,4},{1,5},{2,6},{3,7},{4,0},{5,1},{6,2},{7,3},{8,12},{9,13},{10,... | collective-permute-start | bytes 786440 | tf_op jit(solution)/shard_map/ppermute | solution.py:105
  37.9 0.3 collective-permute-start.16
  38.2 2.8 %collective-permute-done.21.refs_9_ = bf16[512,256]{1,0:T(8,128)(2,1)S(1)} collective-permute-done((bf16[512,256]{1,0:T(8,128)(2,1)S(1)}, bf16[512,256]{1,0:T(8,128)(2,1)S(1)}, u32[]{:S(2)}, u32[]{:S(2)}) %collective-permute-start.21) | collective-permute-done | bytes 262176 | tf_op jit(solution)/shard_map/ppermute | solution.py:101
  41.0 4.8 %collective-permute-start.23 = (bf16[512,256]{1,0:T(8,128)(2,1)S(1)}, bf16[512,256]{1,0:T(8,128)(2,1)S(1)}, u32[]{:S(2)}, u32[]{:S(2)}) collective-permute-start(bf16[512,256]{1,0:T(8,128)(2,1)S(1)} %collective-permute-done.21.refs_9_), channel_id=1, source_target_pairs={{0,8},{8,0},{16,24},{24,16},{1,9},{9,1},{17,25},{25,17},{2,10},{10... | collective-permute-start | bytes 786440 | tf_op jit(solution)/shard_map/ppermute | solution.py:101
  45.7 0.4 collective-permute-done.22.refs_10_
  46.1 0.0 collective-permute-start.17
  46.2 0.0 collective-permute-done.14.refs_1_
  46.2 0.5 collective-permute-start.18
  46.6 0.0 collective-permute-done.15.refs_2_
  46.6 0.1 collective-permute-start.19
  46.7 3.2 %collective-permute-done.16.refs_3_ = bf16[512,256]{1,0:T(8,128)(2,1)S(1)} collective-permute-done((bf16[512,256]{1,0:T(8,128)(2,1)S(1)}, bf16[512,256]{1,0:T(8,128)(2,1)S(1)}, u32[]{:S(2)}, u32[]{:S(2)}) %collective-permute-start.16) | collective-permute-done | bytes 262176 | tf_op jit(solution)/shard_map/ppermute | solution.py:105
  49.9 0.0 collective-permute-start.20
  49.9 2.0 %collective-permute-done.23.refs_11_ = bf16[512,256]{1,0:T(8,128)(2,1)S(1)} collective-permute-done((bf16[512,256]{1,0:T(8,128)(2,1)S(1)}, bf16[512,256]{1,0:T(8,128)(2,1)S(1)}, u32[]{:S(2)}, u32[]{:S(2)}) %collective-permute-start.23) | collective-permute-done | bytes 262176 | tf_op jit(solution)/shard_map/ppermute | solution.py:101
  51.9 0.0 collective-permute-done.17.refs_4_
  51.9 0.0 collective-permute-done.18.refs_5_
  51.9 0.0 collective-permute-done.19.refs_6_
  52.0 0.0 collective-permute-done.20.refs_7_
  52.0 1.5 %product.3 = bf16[512,256]{1,0:T(8,128)(2,1)} custom-call(bf16[512,256]{1,0:T(8,128)(2,1)S(1)} %product.2.refs_0_, bf16[512,256]{1,0:T(8,128)(2,1)S(1)} %collective-permute-done.14.refs_1_, bf16[512,256]{1,0:T(8,128)(2,1)S(1)} %collective-permute-done.15.refs_2_, bf16[512,256]{1,0:T(8,128)(2,1)S(1)} %collective-permute-done.16.refs_3_, ...), custom_call_target="tpu_custom_call" | custom-call | tf_op jit(solution)/shard_map/product/pallas_call | solution.py:87
  (3 shorter events, 0.0 us)
Async XLA Ops:
  0.0 1.2 %copy-start = (bf16[512,1,256]{2,0,1:T(8,128)(2,1)S(1)}, bf16[512,1,256]{2,0,1:T(8,128)(2,1)}, u32[]{:S(2)}) copy-start(bf16[512,1,256]{2,0,1:T(8,128)(2,1)} %param.7) | copy-start | bytes 786436
  1.1 0.7 %copy-start.2 = (s32[1,2,2,2]{3,2,1,0:T(2,128)S(1)}, s32[1,2,2,2]{3,2,1,0:T(2,128)}, u32[]{:S(2)}) copy-start(s32[1,2,2,2]{3,2,1,0:T(2,128)} %h_pat.1) | copy-start | bytes 100
  1.2 0.7 %copy-start.1 = (s32[1,2,2,2]{3,2,1,0:T(2,128)S(1)}, s32[1,2,2,2]{3,2,1,0:T(2,128)}, u32[]{:S(2)}) copy-start(s32[1,2,2,2]{3,2,1,0:T(2,128)} %p_pat.1) | copy-start | bytes 100
  1.2 0.7 %copy-start.3 = (s32[4,1,2]{0,2,1:T(2,128)S(1)}, s32[4,1,2]{0,2,1:T(2,128)}, u32[]{:S(2)}) copy-start(s32[4,1,2]{0,2,1:T(2,128)} %param.10) | copy-start | bytes 100
  2.6 21.6 %collective-permute-start.5 = (bf16[512,256]{1,0:T(8,128)(2,1)S(1)}, bf16[512,256]{1,0:T(8,128)(2,1)S(1)}, u32[]{:S(2)}, u32[]{:S(2)}) collective-permute-start(bf16[512,256]{1,0:T(8,128)(2,1)S(1)} %get-tuple-element.17), channel_id=1, source_target_pairs={{0,1},{1,0},{2,3},{3,2},{4,5},{5,4},{6,7},{7,6},{8,9},{9,8},{10,11... | collective-permute-start | bytes 786440 | tf_op jit(solution)/shard_map/ppermute | solution.py:101
  5.7 7.4 %collective-permute-start = (bf16[256,256]{1,0:T(8,128)(2,1)S(1)}, bf16[256,256]{1,0:T(8,128)(2,1)S(1)}, u32[]{:S(2)}, u32[]{:S(2)}) collective-permute-start(bf16[256,256]{1,0:T(8,128)(2,1)S(1)} %slice.7), channel_id=1, source_target_pairs={{0,9},{1,8},{8,1},{9,0},{16,25},{17,24},{24,17},{25,16},{2,11},{3,... | collective-permute-start | bytes 393224 | tf_op jit(solution)/shard_map/ppermute | solution.py:105
  7.3 6.5 %collective-permute-start.2 = (bf16[256,256]{1,0:T(8,128)(2,1)S(1)}, bf16[256,256]{1,0:T(8,128)(2,1)S(1)}, u32[]{:S(2)}, u32[]{:S(2)}) collective-permute-start(bf16[256,256]{1,0:T(8,128)(2,1)S(1)} %get-tuple-element.19.refs_8_), channel_id=1, source_target_pairs={{0,8},{8,0},{16,24},{24,16},{1,9},{9,1},{17,25},{25,17},{2,10},{10... | collective-permute-start | bytes 393224 | tf_op jit(solution)/shard_map/ppermute | solution.py:101
  7.4 13.5 %collective-permute-start.9 = (bf16[256,256]{1,0:T(8,128)(2,1)S(1)}, bf16[256,256]{1,0:T(8,128)(2,1)S(1)}, u32[]{:S(2)}, u32[]{:S(2)}) collective-permute-start(bf16[256,256]{1,0:T(8,128)(2,1)S(1)} %slice.7), channel_id=1, source_target_pairs={{0,25},{1,24},{8,17},{9,16},{16,9},{17,8},{24,1},{25,0},{2,27},{3,... | collective-permute-start | bytes 393224 | tf_op jit(solution)/shard_map/ppermute | solution.py:105
  12.3 10.1 %collective-permute-start.7 = (bf16[256,256]{1,0:T(8,128)(2,1)S(1)}, bf16[256,256]{1,0:T(8,128)(2,1)S(1)}, u32[]{:S(2)}, u32[]{:S(2)}) collective-permute-start(bf16[256,256]{1,0:T(8,128)(2,1)S(1)} %get-tuple-element.19.refs_8_), channel_id=1, source_target_pairs={{0,24},{8,16},{16,8},{24,0},{1,25},{9,17},{17,9},{25,1},{2,26},{10... | collective-permute-start | bytes 393224 | tf_op jit(solution)/shard_map/ppermute | solution.py:101
  13.1 16.2 %collective-permute-start.1 = (bf16[512,256]{1,0:T(8,128)(2,1)S(1)}, bf16[512,256]{1,0:T(8,128)(2,1)S(1)}, u32[]{:S(2)}, u32[]{:S(2)}) collective-permute-start(bf16[512,256]{1,0:T(8,128)(2,1)S(1)} %get-tuple-element.21.refs_0_), channel_id=1, source_target_pairs={{0,1},{1,0},{2,3},{3,2},{4,5},{5,4},{6,7},{7,6},{8,9},{9,8},{10,11... | collective-permute-start | bytes 786440 | tf_op jit(solution)/shard_map/ppermute | solution.py:105
  13.8 15.5 %collective-permute-start.3 = (bf16[512,256]{1,0:T(8,128)(2,1)S(1)}, bf16[512,256]{1,0:T(8,128)(2,1)S(1)}, u32[]{:S(2)}, u32[]{:S(2)}) collective-permute-start(bf16[512,256]{1,0:T(8,128)(2,1)S(1)} %get-tuple-element.21.refs_0_), channel_id=1, source_target_pairs={{0,4},{1,5},{2,6},{3,7},{4,0},{5,1},{6,2},{7,3},{8,12},{9,13},{10,... | collective-permute-start | bytes 786440 | tf_op jit(solution)/shard_map/ppermute | solution.py:105
  20.9 8.9 %collective-permute-start.4 = (bf16[512,256]{1,0:T(8,128)(2,1)S(1)}, bf16[512,256]{1,0:T(8,128)(2,1)S(1)}, u32[]{:S(2)}, u32[]{:S(2)}) collective-permute-start(bf16[512,256]{1,0:T(8,128)(2,1)S(1)} %get-tuple-element.21.refs_0_), channel_id=1, source_target_pairs={{0,5},{1,4},{2,7},{3,6},{4,1},{5,0},{6,3},{7,2},{8,13},{9,12},{10,... | collective-permute-start | bytes 786440 | tf_op jit(solution)/shard_map/ppermute | solution.py:105
  22.3 5.0 %collective-permute-start.8 = (bf16[256,256]{1,0:T(8,128)(2,1)S(1)}, bf16[256,256]{1,0:T(8,128)(2,1)S(1)}, u32[]{:S(2)}, u32[]{:S(2)}) collective-permute-start(bf16[256,256]{1,0:T(8,128)(2,1)S(1)} %collective-permute-done.7.refs_10_), channel_id=1, source_target_pairs={{0,8},{8,0},{16,24},{24,16},{1,9},{9,1},{17,25},{25,17},{2,10},{10... | collective-permute-start | bytes 393224 | tf_op jit(solution)/shard_map/ppermute | solution.py:101
  24.3 5.0 %collective-permute-start.10 = (bf16[256,256]{1,0:T(8,128)(2,1)S(1)}, bf16[256,256]{1,0:T(8,128)(2,1)S(1)}, u32[]{:S(2)}, u32[]{:S(2)}) collective-permute-start(bf16[256,256]{1,0:T(8,128)(2,1)S(1)} %collective-permute-done.9.refs_13_), channel_id=1, source_target_pairs={{0,8},{8,0},{16,24},{24,16},{1,9},{9,1},{17,25},{25,17},{2,10},{10... | collective-permute-start | bytes 393224 | tf_op jit(solution)/shard_map/ppermute | solution.py:101
  27.3 5.7 %collective-permute-start.6 = (bf16[512,256]{1,0:T(8,128)(2,1)S(1)}, bf16[512,256]{1,0:T(8,128)(2,1)S(1)}, u32[]{:S(2)}, u32[]{:S(2)}) collective-permute-start(bf16[512,256]{1,0:T(8,128)(2,1)S(1)} %get-tuple-element.21.refs_0_), channel_id=1, source_target_pairs={{0,2},{2,0},{4,6},{6,4},{1,3},{3,1},{5,7},{7,5},{8,10},{10,8},{12,... | collective-permute-start | bytes 786440 | tf_op jit(solution)/shard_map/ppermute | solution.py:101
  29.3 3.9 %collective-permute-start.11 = (bf16[512,256]{1,0:T(8,128)(2,1)S(1)}, bf16[512,256]{1,0:T(8,128)(2,1)S(1)}, u32[]{:S(2)}, u32[]{:S(2)}) collective-permute-start(bf16[512,256]{1,0:T(8,128)(2,1)S(1)} %collective-permute-done.1.refs_1_), channel_id=1, source_target_pairs={{0,2},{2,0},{4,6},{6,4},{1,3},{3,1},{5,7},{7,5},{8,10},{10,8},{12,... | collective-permute-start | bytes 786440 | tf_op jit(solution)/shard_map/ppermute | solution.py:101
  29.3 3.9 %collective-permute-start.12 = (bf16[512,256]{1,0:T(8,128)(2,1)S(1)}, bf16[512,256]{1,0:T(8,128)(2,1)S(1)}, u32[]{:S(2)}, u32[]{:S(2)}) collective-permute-start(bf16[512,256]{1,0:T(8,128)(2,1)S(1)} %collective-permute-done.3.refs_2_), channel_id=1, source_target_pairs={{0,2},{2,0},{4,6},{6,4},{1,3},{3,1},{5,7},{7,5},{8,10},{10,8},{12,... | collective-permute-start | bytes 786440 | tf_op jit(solution)/shard_map/ppermute | solution.py:101
  29.8 3.4 %collective-permute-start.13 = (bf16[512,256]{1,0:T(8,128)(2,1)S(1)}, bf16[512,256]{1,0:T(8,128)(2,1)S(1)}, u32[]{:S(2)}, u32[]{:S(2)}) collective-permute-start(bf16[512,256]{1,0:T(8,128)(2,1)S(1)} %collective-permute-done.4.refs_3_), channel_id=1, source_target_pairs={{0,2},{2,0},{4,6},{6,4},{1,3},{3,1},{5,7},{7,5},{8,10},{10,8},{12,... | collective-permute-start | bytes 786440 | tf_op jit(solution)/shard_map/ppermute | solution.py:101
  29.9 3.3 %copy-start.4 = (s32[4,1,2]{0,2,1:T(2,128)S(1)}, s32[4,1,2]{0,2,1:T(2,128)}, u32[]{:S(2)}) copy-start(s32[4,1,2]{0,2,1:T(2,128)} %param.13) | copy-start | bytes 100
  29.9 11.1 %collective-permute-start.21 = (bf16[512,256]{1,0:T(8,128)(2,1)S(1)}, bf16[512,256]{1,0:T(8,128)(2,1)S(1)}, u32[]{:S(2)}, u32[]{:S(2)}) collective-permute-start(bf16[512,256]{1,0:T(8,128)(2,1)S(1)} %pad_maximum_fusion.refs_8_), channel_id=1, source_target_pairs={{0,24},{8,16},{16,8},{24,0},{1,25},{9,17},{17,9},{25,1},{2,26},{10... | collective-permute-start | bytes 786440 | tf_op jit(solution)/shard_map/ppermute | solution.py:101
  33.0 13.1 %collective-permute-start.22 = (bf16[512,256]{1,0:T(8,128)(2,1)S(1)}, bf16[512,256]{1,0:T(8,128)(2,1)S(1)}, u32[]{:S(2)}, u32[]{:S(2)}) collective-permute-start(bf16[512,256]{1,0:T(8,128)(2,1)S(1)} %pad_maximum_fusion.refs_8_), channel_id=1, source_target_pairs={{0,8},{8,0},{16,24},{24,16},{1,9},{9,1},{17,25},{25,17},{2,10},{10... | collective-permute-start | bytes 786440 | tf_op jit(solution)/shard_map/ppermute | solution.py:101
  34.6 11.6 %collective-permute-start.14 = (bf16[512,256]{1,0:T(8,128)(2,1)S(1)}, bf16[512,256]{1,0:T(8,128)(2,1)S(1)}, u32[]{:S(2)}, u32[]{:S(2)}) collective-permute-start(bf16[512,256]{1,0:T(8,128)(2,1)S(1)} %product.2.refs_0_), channel_id=1, source_target_pairs={{0,1},{1,0},{2,3},{3,2},{4,5},{5,4},{6,7},{7,6},{8,9},{9,8},{10,11... | collective-permute-start | bytes 786440 | tf_op jit(solution)/shard_map/ppermute | solution.py:105
  36.4 10.2 %collective-permute-start.15 = (bf16[512,256]{1,0:T(8,128)(2,1)S(1)}, bf16[512,256]{1,0:T(8,128)(2,1)S(1)}, u32[]{:S(2)}, u32[]{:S(2)}) collective-permute-start(bf16[512,256]{1,0:T(8,128)(2,1)S(1)} %product.2.refs_0_), channel_id=1, source_target_pairs={{0,4},{1,5},{2,6},{3,7},{4,0},{5,1},{6,2},{7,3},{8,12},{9,13},{10,... | collective-permute-start | bytes 786440 | tf_op jit(solution)/shard_map/ppermute | solution.py:105
  37.9 12.0 %collective-permute-start.16 = (bf16[512,256]{1,0:T(8,128)(2,1)S(1)}, bf16[512,256]{1,0:T(8,128)(2,1)S(1)}, u32[]{:S(2)}, u32[]{:S(2)}) collective-permute-start(bf16[512,256]{1,0:T(8,128)(2,1)S(1)} %product.2.refs_0_), channel_id=1, source_target_pairs={{0,5},{1,4},{2,7},{3,6},{4,1},{5,0},{6,3},{7,2},{8,13},{9,12},{10,... | collective-permute-start | bytes 786440 | tf_op jit(solution)/shard_map/ppermute | solution.py:105
  41.0 11.0 %collective-permute-start.23 = (bf16[512,256]{1,0:T(8,128)(2,1)S(1)}, bf16[512,256]{1,0:T(8,128)(2,1)S(1)}, u32[]{:S(2)}, u32[]{:S(2)}) collective-permute-start(bf16[512,256]{1,0:T(8,128)(2,1)S(1)} %collective-permute-done.21.refs_9_), channel_id=1, source_target_pairs={{0,8},{8,0},{16,24},{24,16},{1,9},{9,1},{17,25},{25,17},{2,10},{10... | collective-permute-start | bytes 786440 | tf_op jit(solution)/shard_map/ppermute | solution.py:101
  46.1 5.8 %collective-permute-start.17 = (bf16[512,256]{1,0:T(8,128)(2,1)S(1)}, bf16[512,256]{1,0:T(8,128)(2,1)S(1)}, u32[]{:S(2)}, u32[]{:S(2)}) collective-permute-start(bf16[512,256]{1,0:T(8,128)(2,1)S(1)} %product.2.refs_0_), channel_id=1, source_target_pairs={{0,2},{2,0},{4,6},{6,4},{1,3},{3,1},{5,7},{7,5},{8,10},{10,8},{12,... | collective-permute-start | bytes 786440 | tf_op jit(solution)/shard_map/ppermute | solution.py:101
  46.2 5.8 %collective-permute-start.18 = (bf16[512,256]{1,0:T(8,128)(2,1)S(1)}, bf16[512,256]{1,0:T(8,128)(2,1)S(1)}, u32[]{:S(2)}, u32[]{:S(2)}) collective-permute-start(bf16[512,256]{1,0:T(8,128)(2,1)S(1)} %collective-permute-done.14.refs_1_), channel_id=1, source_target_pairs={{0,2},{2,0},{4,6},{6,4},{1,3},{3,1},{5,7},{7,5},{8,10},{10,8},{12,... | collective-permute-start | bytes 786440 | tf_op jit(solution)/shard_map/ppermute | solution.py:101
  46.6 5.3 %collective-permute-start.19 = (bf16[512,256]{1,0:T(8,128)(2,1)S(1)}, bf16[512,256]{1,0:T(8,128)(2,1)S(1)}, u32[]{:S(2)}, u32[]{:S(2)}) collective-permute-start(bf16[512,256]{1,0:T(8,128)(2,1)S(1)} %collective-permute-done.15.refs_2_), channel_id=1, source_target_pairs={{0,2},{2,0},{4,6},{6,4},{1,3},{3,1},{5,7},{7,5},{8,10},{10,8},{12,... | collective-permute-start | bytes 786440 | tf_op jit(solution)/shard_map/ppermute | solution.py:101
  49.9 2.0 %collective-permute-start.20 = (bf16[512,256]{1,0:T(8,128)(2,1)S(1)}, bf16[512,256]{1,0:T(8,128)(2,1)S(1)}, u32[]{:S(2)}, u32[]{:S(2)}) collective-permute-start(bf16[512,256]{1,0:T(8,128)(2,1)S(1)} %collective-permute-done.16.refs_3_), channel_id=1, source_target_pairs={{0,2},{2,0},{4,6},{6,4},{1,3},{3,1},{5,7},{7,5},{8,10},{10,8},{12,... | collective-permute-start | bytes 786440 | tf_op jit(solution)/shard_map/ppermute | solution.py:101

commit v3 on v2

--- a/solution.py
+++ b/solution.py
@@ -110,16 +110,16 @@
 
 
 WAITS = {
-    "s20": ("p1",),
-    "sc00": ("ph",),
-    "sc01": ("p2", "q2", "q1", "ph",),
-    "sc20": ("p2", "q2", "ph",),
+    "s20": ("p1", "s01",),
+    "sc00": ("p3",),
+    "sc01": ("p2", "ph", "q1", "q2",),
+    "sc20": ("p2", "ph", "q2", "s20",),
     "sc21": ("p2", "q2",),
-    "q2": ("ph",),
-    "s01": ("q1",),
+    "q2": ("s01",),
+    "ph": ("p3",),
 }
 ORDER = (
-    "ph", "p3", "sc00", "p1", "q1", "s21", "q3", "s01", "s20", "p2", "q2", "h3", "h1", "sc01", "sc20",
+    "s01", "p3", "ph", "p1", "q1", "q3", "s20", "s21", "sc00", "p2", "q2", "h3", "h1", "sc01", "sc20",
     "sc21", "x", "x21", "x01", "x20", "h2", "xc00", "xc01", "xc20", "xc21",
 )
 
@@ -170,6 +170,8 @@
         return {(0, 0): own, **{m: done[f"{kind}{m[0]}{m[1]}"] for m in plane}}
 
     def between(kind, own, m):
+        if kind == "s" and m[0] and m[1]:
+            return lambda: ex.add(f"s{m[0]}{m[1]}", done["s01"], ("col",), (m[0],))
         return lambda: ex.add(f"{kind}{m[0]}{m[1]}", own(), ("col", "layer"), m)
 
     def cores(kind, own, m):

time: 53.6 us -> 52 us (0.970)
  starting transfers between devices: 27.7 us -> 23 us
  waiting for transfers between devices: 20.1 us -> 23.1 us
    ppermute x16 -> x17, waiting for transfers between devices: 10.7 us -> 20.6 us  [exchange(): lax.ppermute(value, axes[0], [(i, i ^ mask[0]) for i in range(sizes[0])])]
    ppermute x8 -> x7, waiting for transfers between devices: 9.42 us -> 2.53 us  [exchange(): return lax.ppermute(value, axes, pairs)]
    ppermute x8 -> x7, starting transfers between devices: 13 us -> 10.4 us  [exchange(): return lax.ppermute(value, axes, pairs)]
    ppermute x16 -> x17, starting transfers between devices: 14.6 us -> 12.6 us  [exchange(): lax.ppermute(value, axes[0], [(i, i ^ mask[0]) for i in range(sizes[0])])]
  transfers between devices with their start and end apart: 24 -> 24, of which waited for: 9 -> 10; matrix products, arithmetic and copies ran while one was open for 0% -> 0% of each run, Pallas kernels for 3% -> 3%
where the time goes in v3:
time: 52 us; the launch traced here: 51.8 us
  waiting for transfers between devices  23.1 us (44%)
  starting transfers between devices  23 us (44%)
  Pallas kernels  3.68 us (7%)
  local copies, waits for them, and re-layouts  1.85 us (4%)
    ppermute x17, waiting for transfers between devices, exchange(): lax.ppermute(value, axes[0], [(i, i ^ mask[0]) for i in range(sizes[0])])  20.6 us
    ppermute x17, starting transfers between devices, exchange(): lax.ppermute(value, axes[0], [(i, i ^ mask[0]) for i in range(sizes[0])])  12.6 us
    ppermute x7, starting transfers between devices, exchange(): return lax.ppermute(value, axes, pairs)  10.4 us
    pallas_call x2, Pallas kernels, product(): pl.pallas_call(kernel, out_shape=jax.ShapeDtypeStruct((rows, cols), jnp.b...  2.9 us
    ppermute x7, waiting for transfers between devices, exchange(): return lax.ppermute(value, axes, pairs)  2.53 us
    transpose x1, local copies, waits for them, and re-layouts, mask_all(): h[0].transpose(1, 0, 2)  1.14 us
  transfers between devices with their start and end apart: 24, of which 10 were waited for; matrix products, arithmetic and copies ran while one was open for 0% of the time, Pallas kernels for 3%

profile of v3, /device:TPU:0, one launch (start us, length us, event | category | flops | bytes accessed | tf_op | source)
XLA Modules:
  0.0 51.8 jit_solution(11766504695548036324)
XLA Ops:
  0.0 0.0 copy-start
  0.0 1.1 %copy_bitcast_fusion = (bf16[2,256,256]{2,1,0:T(8,128)(2,1)S(1)}, bf16[2,256,256]{2,1,0:T(8,128)(2,1)S(1)}) fusion(bf16[1,256,2,256]{3,2,1,0:T(2,128)(2,1)} %param.9, bf16[1,256,2,256]{3,2,1,0:T(2,128)(2,1)} %param.8), kind=kLoop, calls=%fused_computation.1 | loop fusion | bytes 1048576 | tf_op jit(solution)/shard_map/transpose | solution.py:56
  1.1 0.0 copy-start.2
  1.2 0.0 copy-start.1
  1.2 0.0 copy-start.3
  1.2 0.0 copy-done
  1.2 0.6 %copy-done.2 = s32[1,2,2,2]{3,2,1,0:T(2,128)S(1)} copy-done((s32[1,2,2,2]{3,2,1,0:T(2,128)S(1)}, s32[1,2,2,2]{3,2,1,0:T(2,128)}, u32[]{:S(2)}) %copy-start.2) | copy-done | bytes 56
  1.8 0.0 copy-done.1
  1.9 0.0 copy-done.3
  1.9 0.8 %mask_all.1 = (bf16[512,256]{1,0:T(8,128)(2,1)S(1)}, bf16[256,256]{1,0:T(8,128)(2,1)S(1)}, bf16[256,256]{1,0:T(8,128)(2,1)S(1)}, bf16[512,256]{1,0:T(8,128)(2,1)S(1)}) custom-call(bf16[512,256]{1,0:T(8,128)(2,1)S(1)} %bitcast.16, bf16[2,256,256]{2,1,0:T(8,128)(2,1)S(1)} %get-tuple-element.28.p_ref, bf16[2,256,256]{2,1,0:T(8,128)(2,1)S(1)} %get-tuple-element.27.h_ref, ...), custom_call_target="tpu_custom_call" | custom-call | tf_op jit(solution)/shard_map/mask_all/pallas_call | solution.py:48
  2.6 3.0 %collective-permute-start = (bf16[512,256]{1,0:T(8,128)(2,1)S(1)}, bf16[512,256]{1,0:T(8,128)(2,1)S(1)}, u32[]{:S(2)}, u32[]{:S(2)}) collective-permute-start(bf16[512,256]{1,0:T(8,128)(2,1)S(1)} %get-tuple-element.19.refs_0_), channel_id=1, source_target_pairs={{0,1},{1,0},{2,3},{3,2},{4,5},{5,4},{6,7},{7,6},{8,9},{9,8},{10,11... | collective-permute-start | bytes 786440 | tf_op jit(solution)/shard_map/ppermute | solution.py:105
  5.7 3.6 %collective-permute-start.4 = (bf16[256,256]{1,0:T(8,128)(2,1)S(1)}, bf16[256,256]{1,0:T(8,128)(2,1)S(1)}, u32[]{:S(2)}, u32[]{:S(2)}) collective-permute-start(bf16[256,256]{1,0:T(8,128)(2,1)S(1)} %get-tuple-element.17.refs_8_), channel_id=1, source_target_pairs={{0,24},{8,16},{16,8},{24,0},{1,25},{9,17},{17,9},{25,1},{2,26},{10... | collective-permute-start | bytes 393224 | tf_op jit(solution)/shard_map/ppermute | solution.py:101
  9.3 0.0 collective-permute-start.1
  9.3 0.9 %collective-permute-start.9 = (bf16[256,256]{1,0:T(8,128)(2,1)S(1)}, bf16[256,256]{1,0:T(8,128)(2,1)S(1)}, u32[]{:S(2)}, u32[]{:S(2)}) collective-permute-start(bf16[256,256]{1,0:T(8,128)(2,1)S(1)} %slice.7), channel_id=1, source_target_pairs={{0,25},{1,24},{8,17},{9,16},{16,9},{17,8},{24,1},{25,0},{2,27},{3,... | collective-permute-start | bytes 393224 | tf_op jit(solution)/shard_map/ppermute | solution.py:105
  10.2 1.4 %collective-permute-start.8 = (bf16[256,256]{1,0:T(8,128)(2,1)S(1)}, bf16[256,256]{1,0:T(8,128)(2,1)S(1)}, u32[]{:S(2)}, u32[]{:S(2)}) collective-permute-start(bf16[256,256]{1,0:T(8,128)(2,1)S(1)} %slice.7), channel_id=1, source_target_pairs={{0,9},{1,8},{8,1},{9,0},{16,25},{17,24},{24,17},{25,16},{2,11},{3,... | collective-permute-start | bytes 393224 | tf_op jit(solution)/shard_map/ppermute | solution.py:105
  11.6 2.3 %collective-permute-done.4.refs_10_ = bf16[256,256]{1,0:T(8,128)(2,1)S(1)} collective-permute-done((bf16[256,256]{1,0:T(8,128)(2,1)S(1)}, bf16[256,256]{1,0:T(8,128)(2,1)S(1)}, u32[]{:S(2)}, u32[]{:S(2)}) %collective-permute-start.4) | collective-permute-done | bytes 131104 | tf_op jit(solution)/shard_map/ppermute | solution.py:101
  13.9 0.3 collective-permute-start.7
  14.2 4.4 %collective-permute-done.1.refs_11_ = bf16[256,256]{1,0:T(8,128)(2,1)S(1)} collective-permute-done((bf16[256,256]{1,0:T(8,128)(2,1)S(1)}, bf16[256,256]{1,0:T(8,128)(2,1)S(1)}, u32[]{:S(2)}, u32[]{:S(2)}) %collective-permute-start.1) | collective-permute-done | bytes 131104 | tf_op jit(solution)/shard_map/ppermute | solution.py:101
  18.6 0.0 collective-permute-done.refs_1_
  18.6 1.5 %collective-permute-start.2 = (bf16[512,256]{1,0:T(8,128)(2,1)S(1)}, bf16[512,256]{1,0:T(8,128)(2,1)S(1)}, u32[]{:S(2)}, u32[]{:S(2)}) collective-permute-start(bf16[512,256]{1,0:T(8,128)(2,1)S(1)} %get-tuple-element.19.refs_0_), channel_id=1, source_target_pairs={{0,4},{1,5},{2,6},{3,7},{4,0},{5,1},{6,2},{7,3},{8,12},{9,13},{10,... | collective-permute-start | bytes 786440 | tf_op jit(solution)/shard_map/ppermute | solution.py:105
  20.1 0.5 %collective-permute-start.3 = (bf16[512,256]{1,0:T(8,128)(2,1)S(1)}, bf16[512,256]{1,0:T(8,128)(2,1)S(1)}, u32[]{:S(2)}, u32[]{:S(2)}) collective-permute-start(bf16[512,256]{1,0:T(8,128)(2,1)S(1)} %collective-permute-done.refs_1_), channel_id=1, source_target_pairs={{0,4},{2,6},{4,0},{6,2},{1,5},{3,7},{5,1},{7,3},{8,12},{10,14},{12... | collective-permute-start | bytes 786440 | tf_op jit(solution)/shard_map/ppermute | solution.py:101
  20.6 0.0 collective-permute-done.9.refs_13_
  20.6 0.5 collective-permute-start.6
  21.1 0.0 collective-permute-done.8.refs_14_
  21.1 1.7 %collective-permute-start.10 = (bf16[256,256]{1,0:T(8,128)(2,1)S(1)}, bf16[256,256]{1,0:T(8,128)(2,1)S(1)}, u32[]{:S(2)}, u32[]{:S(2)}) collective-permute-start(bf16[256,256]{1,0:T(8,128)(2,1)S(1)} %collective-permute-done.9.refs_13_), channel_id=1, source_target_pairs={{0,8},{8,0},{16,24},{24,16},{1,9},{9,1},{17,25},{25,17},{2,10},{10... | collective-permute-start | bytes 393224 | tf_op jit(solution)/shard_map/ppermute | solution.py:101
  22.8 2.9 %collective-permute-done.6.refs_12_ = bf16[256,256]{1,0:T(8,128)(2,1)S(1)} collective-permute-done((bf16[256,256]{1,0:T(8,128)(2,1)S(1)}, bf16[256,256]{1,0:T(8,128)(2,1)S(1)}, u32[]{:S(2)}, u32[]{:S(2)}) %collective-permute-start.6) | collective-permute-done | bytes 131104 | tf_op jit(solution)/shard_map/ppermute | solution.py:101
  25.8 0.0 collective-permute-start.5
  25.8 1.4 %collective-permute-done.10.refs_15_ = bf16[256,256]{1,0:T(8,128)(2,1)S(1)} collective-permute-done((bf16[256,256]{1,0:T(8,128)(2,1)S(1)}, bf16[256,256]{1,0:T(8,128)(2,1)S(1)}, u32[]{:S(2)}, u32[]{:S(2)}) %collective-permute-start.10) | collective-permute-done | bytes 131104 | tf_op jit(solution)/shard_map/ppermute | solution.py:101
  27.2 0.0 collective-permute-done.7.refs_9_
  27.2 0.0 collective-permute-start.11
  27.2 0.0 collective-permute-done.2.refs_2_
  27.2 0.5 collective-permute-start.12
  27.7 1.4 %collective-permute-done.3.refs_3_ = bf16[512,256]{1,0:T(8,128)(2,1)S(1)} collective-permute-done((bf16[512,256]{1,0:T(8,128)(2,1)S(1)}, bf16[512,256]{1,0:T(8,128)(2,1)S(1)}, u32[]{:S(2)}, u32[]{:S(2)}) %collective-permute-start.3) | collective-permute-done | bytes 262176 | tf_op jit(solution)/shard_map/ppermute | solution.py:101
  29.1 0.0 collective-permute-start.13
  29.1 0.0 copy-start.4
  29.1 1.0 %collective-permute-start.21 = (bf16[512,256]{1,0:T(8,128)(2,1)S(1)}, bf16[512,256]{1,0:T(8,128)(2,1)S(1)}, u32[]{:S(2)}, u32[]{:S(2)}) collective-permute-start(bf16[512,256]{1,0:T(8,128)(2,1)S(1)} %pad_maximum_fusion.refs_8_), channel_id=1, source_target_pairs={{0,24},{8,16},{16,8},{24,0},{1,25},{9,17},{17,9},{25,1},{2,26},{10... | collective-permute-start | bytes 786440 | tf_op jit(solution)/shard_map/ppermute | solution.py:101
  30.1 0.0 collective-permute-done.5.refs_4_
  30.1 0.0 collective-permute-start.22
  30.1 0.0 collective-permute-done.11.refs_5_
  30.1 0.0 collective-permute-done.12.refs_6_
  30.2 0.5 collective-permute-done.13.refs_7_
  30.6 0.0 copy-done.4
  30.6 1.4 %product.2.refs_0_ = bf16[512,256]{1,0:T(8,128)(2,1)S(1)} custom-call(bf16[512,256]{1,0:T(8,128)(2,1)S(1)} %get-tuple-element.19.refs_0_, bf16[512,256]{1,0:T(8,128)(2,1)S(1)} %collective-permute-done.refs_1_, bf16[512,256]{1,0:T(8,128)(2,1)S(1)} %collective-permute-done.2.refs_2_, bf16[512,256]{1,0:T(8,128)(2,1)S(1)} %collective-permute-done.3.refs_3_, ...), custom_call_target="tpu_custom_call" | custom-call | tf_op jit(solution)/shard_map/product/pallas_call | solution.py:87
  32.0 1.1 %collective-permute-start.14 = (bf16[512,256]{1,0:T(8,128)(2,1)S(1)}, bf16[512,256]{1,0:T(8,128)(2,1)S(1)}, u32[]{:S(2)}, u32[]{:S(2)}) collective-permute-start(bf16[512,256]{1,0:T(8,128)(2,1)S(1)} %product.2.refs_0_), channel_id=1, source_target_pairs={{0,1},{1,0},{2,3},{3,2},{4,5},{5,4},{6,7},{7,6},{8,9},{9,8},{10,11... | collective-permute-start | bytes 786440 | tf_op jit(solution)/shard_map/ppermute | solution.py:105
  33.2 1.5 %collective-permute-start.15 = (bf16[512,256]{1,0:T(8,128)(2,1)S(1)}, bf16[512,256]{1,0:T(8,128)(2,1)S(1)}, u32[]{:S(2)}, u32[]{:S(2)}) collective-permute-start(bf16[512,256]{1,0:T(8,128)(2,1)S(1)} %product.2.refs_0_), channel_id=1, source_target_pairs={{0,4},{1,5},{2,6},{3,7},{4,0},{5,1},{6,2},{7,3},{8,12},{9,13},{10,... | collective-permute-start | bytes 786440 | tf_op jit(solution)/shard_map/ppermute | solution.py:105
  34.7 0.9 %collective-permute-start.16 = (bf16[512,256]{1,0:T(8,128)(2,1)S(1)}, bf16[512,256]{1,0:T(8,128)(2,1)S(1)}, u32[]{:S(2)}, u32[]{:S(2)}) collective-permute-start(bf16[512,256]{1,0:T(8,128)(2,1)S(1)} %product.2.refs_0_), channel_id=1, source_target_pairs={{0,5},{1,4},{2,7},{3,6},{4,1},{5,0},{6,3},{7,2},{8,13},{9,12},{10,... | collective-permute-start | bytes 786440 | tf_op jit(solution)/shard_map/ppermute | solution.py:105
  35.6 4.6 %collective-permute-done.21.refs_9_ = bf16[512,256]{1,0:T(8,128)(2,1)S(1)} collective-permute-done((bf16[512,256]{1,0:T(8,128)(2,1)S(1)}, bf16[512,256]{1,0:T(8,128)(2,1)S(1)}, u32[]{:S(2)}, u32[]{:S(2)}) %collective-permute-start.21) | collective-permute-done | bytes 262176 | tf_op jit(solution)/shard_map/ppermute | solution.py:101
  40.2 3.9 %collective-permute-start.23 = (bf16[512,256]{1,0:T(8,128)(2,1)S(1)}, bf16[512,256]{1,0:T(8,128)(2,1)S(1)}, u32[]{:S(2)}, u32[]{:S(2)}) collective-permute-start(bf16[512,256]{1,0:T(8,128)(2,1)S(1)} %collective-permute-done.21.refs_9_), channel_id=1, source_target_pairs={{0,8},{8,0},{16,24},{24,16},{1,9},{9,1},{17,25},{25,17},{2,10},{10... | collective-permute-start | bytes 786440 | tf_op jit(solution)/shard_map/ppermute | solution.py:101
  44.1 0.1 collective-permute-done.22.refs_10_
  44.1 0.0 collective-permute-start.17
  44.1 0.0 collective-permute-done.14.refs_1_
  44.1 0.5 collective-permute-start.18
  44.6 0.0 collective-permute-done.15.refs_2_
  44.6 0.1 collective-permute-start.19
  44.7 2.5 %collective-permute-done.16.refs_3_ = bf16[512,256]{1,0:T(8,128)(2,1)S(1)} collective-permute-done((bf16[512,256]{1,0:T(8,128)(2,1)S(1)}, bf16[512,256]{1,0:T(8,128)(2,1)S(1)}, u32[]{:S(2)}, u32[]{:S(2)}) %collective-permute-start.16) | collective-permute-done | bytes 262176 | tf_op jit(solution)/shard_map/ppermute | solution.py:105
  47.2 0.0 collective-permute-start.20
  47.2 3.0 %collective-permute-done.23.refs_11_ = bf16[512,256]{1,0:T(8,128)(2,1)S(1)} collective-permute-done((bf16[512,256]{1,0:T(8,128)(2,1)S(1)}, bf16[512,256]{1,0:T(8,128)(2,1)S(1)}, u32[]{:S(2)}, u32[]{:S(2)}) %collective-permute-start.23) | collective-permute-done | bytes 262176 | tf_op jit(solution)/shard_map/ppermute | solution.py:101
  50.3 0.0 collective-permute-done.17.refs_4_
  50.3 0.0 collective-permute-done.18.refs_5_
  50.3 0.0 collective-permute-done.19.refs_6_
  50.3 0.0 collective-permute-done.20.refs_7_
  50.3 1.5 %product.3 = bf16[512,256]{1,0:T(8,128)(2,1)} custom-call(bf16[512,256]{1,0:T(8,128)(2,1)S(1)} %product.2.refs_0_, bf16[512,256]{1,0:T(8,128)(2,1)S(1)} %collective-permute-done.14.refs_1_, bf16[512,256]{1,0:T(8,128)(2,1)S(1)} %collective-permute-done.15.refs_2_, bf16[512,256]{1,0:T(8,128)(2,1)S(1)} %collective-permute-done.16.refs_3_, ...), custom_call_target="tpu_custom_call" | custom-call | tf_op jit(solution)/shard_map/product/pallas_call | solution.py:87
  (3 shorter events, 0.0 us)
Async XLA Ops:
  0.0 1.2 %copy-start = (bf16[512,1,256]{2,0,1:T(8,128)(2,1)S(1)}, bf16[512,1,256]{2,0,1:T(8,128)(2,1)}, u32[]{:S(2)}) copy-start(bf16[512,1,256]{2,0,1:T(8,128)(2,1)} %param.7) | copy-start | bytes 786436
  1.1 0.7 %copy-start.2 = (s32[1,2,2,2]{3,2,1,0:T(2,128)S(1)}, s32[1,2,2,2]{3,2,1,0:T(2,128)}, u32[]{:S(2)}) copy-start(s32[1,2,2,2]{3,2,1,0:T(2,128)} %h_pat.1) | copy-start | bytes 100
  1.2 0.7 %copy-start.1 = (s32[1,2,2,2]{3,2,1,0:T(2,128)S(1)}, s32[1,2,2,2]{3,2,1,0:T(2,128)}, u32[]{:S(2)}) copy-start(s32[1,2,2,2]{3,2,1,0:T(2,128)} %p_pat.1) | copy-start | bytes 100
  1.2 0.7 %copy-start.3 = (s32[4,1,2]{0,2,1:T(2,128)S(1)}, s32[4,1,2]{0,2,1:T(2,128)}, u32[]{:S(2)}) copy-start(s32[4,1,2]{0,2,1:T(2,128)} %param.10) | copy-start | bytes 100
  2.6 15.9 %collective-permute-start = (bf16[512,256]{1,0:T(8,128)(2,1)S(1)}, bf16[512,256]{1,0:T(8,128)(2,1)S(1)}, u32[]{:S(2)}, u32[]{:S(2)}) collective-permute-start(bf16[512,256]{1,0:T(8,128)(2,1)S(1)} %get-tuple-element.19.refs_0_), channel_id=1, source_target_pairs={{0,1},{1,0},{2,3},{3,2},{4,5},{5,4},{6,7},{7,6},{8,9},{9,8},{10,11... | collective-permute-start | bytes 786440 | tf_op jit(solution)/shard_map/ppermute | solution.py:105
  5.7 8.2 %collective-permute-start.4 = (bf16[256,256]{1,0:T(8,128)(2,1)S(1)}, bf16[256,256]{1,0:T(8,128)(2,1)S(1)}, u32[]{:S(2)}, u32[]{:S(2)}) collective-permute-start(bf16[256,256]{1,0:T(8,128)(2,1)S(1)} %get-tuple-element.17.refs_8_), channel_id=1, source_target_pairs={{0,24},{8,16},{16,8},{24,0},{1,25},{9,17},{17,9},{25,1},{2,26},{10... | collective-permute-start | bytes 393224 | tf_op jit(solution)/shard_map/ppermute | solution.py:101
  9.3 9.3 %collective-permute-start.1 = (bf16[256,256]{1,0:T(8,128)(2,1)S(1)}, bf16[256,256]{1,0:T(8,128)(2,1)S(1)}, u32[]{:S(2)}, u32[]{:S(2)}) collective-permute-start(bf16[256,256]{1,0:T(8,128)(2,1)S(1)} %get-tuple-element.17.refs_8_), channel_id=1, source_target_pairs={{0,8},{8,0},{16,24},{24,16},{1,9},{9,1},{17,25},{25,17},{2,10},{10... | collective-permute-start | bytes 393224 | tf_op jit(solution)/shard_map/ppermute | solution.py:101
  9.3 11.3 %collective-permute-start.9 = (bf16[256,256]{1,0:T(8,128)(2,1)S(1)}, bf16[256,256]{1,0:T(8,128)(2,1)S(1)}, u32[]{:S(2)}, u32[]{:S(2)}) collective-permute-start(bf16[256,256]{1,0:T(8,128)(2,1)S(1)} %slice.7), channel_id=1, source_target_pairs={{0,25},{1,24},{8,17},{9,16},{16,9},{17,8},{24,1},{25,0},{2,27},{3,... | collective-permute-start | bytes 393224 | tf_op jit(solution)/shard_map/ppermute | solution.py:105
  10.2 10.9 %collective-permute-start.8 = (bf16[256,256]{1,0:T(8,128)(2,1)S(1)}, bf16[256,256]{1,0:T(8,128)(2,1)S(1)}, u32[]{:S(2)}, u32[]{:S(2)}) collective-permute-start(bf16[256,256]{1,0:T(8,128)(2,1)S(1)} %slice.7), channel_id=1, source_target_pairs={{0,9},{1,8},{8,1},{9,0},{16,25},{17,24},{24,17},{25,16},{2,11},{3,... | collective-permute-start | bytes 393224 | tf_op jit(solution)/shard_map/ppermute | solution.py:105
  13.9 13.3 %collective-permute-start.7 = (bf16[512,256]{1,0:T(8,128)(2,1)S(1)}, bf16[512,256]{1,0:T(8,128)(2,1)S(1)}, u32[]{:S(2)}, u32[]{:S(2)}) collective-permute-start(bf16[512,256]{1,0:T(8,128)(2,1)S(1)} %get-tuple-element.21), channel_id=1, source_target_pairs={{0,1},{1,0},{2,3},{3,2},{4,5},{5,4},{6,7},{7,6},{8,9},{9,8},{10,11... | collective-permute-start | bytes 786440 | tf_op jit(solution)/shard_map/ppermute | solution.py:101
  18.6 8.6 %collective-permute-start.2 = (bf16[512,256]{1,0:T(8,128)(2,1)S(1)}, bf16[512,256]{1,0:T(8,128)(2,1)S(1)}, u32[]{:S(2)}, u32[]{:S(2)}) collective-permute-start(bf16[512,256]{1,0:T(8,128)(2,1)S(1)} %get-tuple-element.19.refs_0_), channel_id=1, source_target_pairs={{0,4},{1,5},{2,6},{3,7},{4,0},{5,1},{6,2},{7,3},{8,12},{9,13},{10,... | collective-permute-start | bytes 786440 | tf_op jit(solution)/shard_map/ppermute | solution.py:105
  20.1 9.0 %collective-permute-start.3 = (bf16[512,256]{1,0:T(8,128)(2,1)S(1)}, bf16[512,256]{1,0:T(8,128)(2,1)S(1)}, u32[]{:S(2)}, u32[]{:S(2)}) collective-permute-start(bf16[512,256]{1,0:T(8,128)(2,1)S(1)} %collective-permute-done.refs_1_), channel_id=1, source_target_pairs={{0,4},{2,6},{4,0},{6,2},{1,5},{3,7},{5,1},{7,3},{8,12},{10,14},{12... | collective-permute-start | bytes 786440 | tf_op jit(solution)/shard_map/ppermute | solution.py:101
  20.6 5.2 %collective-permute-start.6 = (bf16[256,256]{1,0:T(8,128)(2,1)S(1)}, bf16[256,256]{1,0:T(8,128)(2,1)S(1)}, u32[]{:S(2)}, u32[]{:S(2)}) collective-permute-start(bf16[256,256]{1,0:T(8,128)(2,1)S(1)} %collective-permute-done.4.refs_10_), channel_id=1, source_target_pairs={{0,8},{8,0},{16,24},{24,16},{1,9},{9,1},{17,25},{25,17},{2,10},{10... | collective-permute-start | bytes 393224 | tf_op jit(solution)/shard_map/ppermute | solution.py:101
  21.1 6.1 %collective-permute-start.10 = (bf16[256,256]{1,0:T(8,128)(2,1)S(1)}, bf16[256,256]{1,0:T(8,128)(2,1)S(1)}, u32[]{:S(2)}, u32[]{:S(2)}) collective-permute-start(bf16[256,256]{1,0:T(8,128)(2,1)S(1)} %collective-permute-done.9.refs_13_), channel_id=1, source_target_pairs={{0,8},{8,0},{16,24},{24,16},{1,9},{9,1},{17,25},{25,17},{2,10},{10... | collective-permute-start | bytes 393224 | tf_op jit(solution)/shard_map/ppermute | solution.py:101
  25.8 4.4 %collective-permute-start.5 = (bf16[512,256]{1,0:T(8,128)(2,1)S(1)}, bf16[512,256]{1,0:T(8,128)(2,1)S(1)}, u32[]{:S(2)}, u32[]{:S(2)}) collective-permute-start(bf16[512,256]{1,0:T(8,128)(2,1)S(1)} %get-tuple-element.19.refs_0_), channel_id=1, source_target_pairs={{0,2},{2,0},{4,6},{6,4},{1,3},{3,1},{5,7},{7,5},{8,10},{10,8},{12,... | collective-permute-start | bytes 786440 | tf_op jit(solution)/shard_map/ppermute | solution.py:101
  27.2 3.0 %collective-permute-start.11 = (bf16[512,256]{1,0:T(8,128)(2,1)S(1)}, bf16[512,256]{1,0:T(8,128)(2,1)S(1)}, u32[]{:S(2)}, u32[]{:S(2)}) collective-permute-start(bf16[512,256]{1,0:T(8,128)(2,1)S(1)} %collective-permute-done.refs_1_), channel_id=1, source_target_pairs={{0,2},{2,0},{4,6},{6,4},{1,3},{3,1},{5,7},{7,5},{8,10},{10,8},{12,... | collective-permute-start | bytes 786440 | tf_op jit(solution)/shard_map/ppermute | solution.py:101
  27.2 3.0 %collective-permute-start.12 = (bf16[512,256]{1,0:T(8,128)(2,1)S(1)}, bf16[512,256]{1,0:T(8,128)(2,1)S(1)}, u32[]{:S(2)}, u32[]{:S(2)}) collective-permute-start(bf16[512,256]{1,0:T(8,128)(2,1)S(1)} %collective-permute-done.2.refs_2_), channel_id=1, source_target_pairs={{0,2},{2,0},{4,6},{6,4},{1,3},{3,1},{5,7},{7,5},{8,10},{10,8},{12,... | collective-permute-start | bytes 786440 | tf_op jit(solution)/shard_map/ppermute | solution.py:101
  29.1 1.5 %collective-permute-start.13 = (bf16[512,256]{1,0:T(8,128)(2,1)S(1)}, bf16[512,256]{1,0:T(8,128)(2,1)S(1)}, u32[]{:S(2)}, u32[]{:S(2)}) collective-permute-start(bf16[512,256]{1,0:T(8,128)(2,1)S(1)} %collective-permute-done.3.refs_3_), channel_id=1, source_target_pairs={{0,2},{2,0},{4,6},{6,4},{1,3},{3,1},{5,7},{7,5},{8,10},{10,8},{12,... | collective-permute-start | bytes 786440 | tf_op jit(solution)/shard_map/ppermute | solution.py:101
  29.1 1.5 %copy-start.4 = (s32[4,1,2]{0,2,1:T(2,128)S(1)}, s32[4,1,2]{0,2,1:T(2,128)}, u32[]{:S(2)}) copy-start(s32[4,1,2]{0,2,1:T(2,128)} %param.13) | copy-start | bytes 100
  29.1 11.0 %collective-permute-start.21 = (bf16[512,256]{1,0:T(8,128)(2,1)S(1)}, bf16[512,256]{1,0:T(8,128)(2,1)S(1)}, u32[]{:S(2)}, u32[]{:S(2)}) collective-permute-start(bf16[512,256]{1,0:T(8,128)(2,1)S(1)} %pad_maximum_fusion.refs_8_), channel_id=1, source_target_pairs={{0,24},{8,16},{16,8},{24,0},{1,25},{9,17},{17,9},{25,1},{2,26},{10... | collective-permute-start | bytes 786440 | tf_op jit(solution)/shard_map/ppermute | solution.py:101
  30.1 14.0 %collective-permute-start.22 = (bf16[512,256]{1,0:T(8,128)(2,1)S(1)}, bf16[512,256]{1,0:T(8,128)(2,1)S(1)}, u32[]{:S(2)}, u32[]{:S(2)}) collective-permute-start(bf16[512,256]{1,0:T(8,128)(2,1)S(1)} %pad_maximum_fusion.refs_8_), channel_id=1, source_target_pairs={{0,8},{8,0},{16,24},{24,16},{1,9},{9,1},{17,25},{25,17},{2,10},{10... | collective-permute-start | bytes 786440 | tf_op jit(solution)/shard_map/ppermute | solution.py:101
  32.0 12.1 %collective-permute-start.14 = (bf16[512,256]{1,0:T(8,128)(2,1)S(1)}, bf16[512,256]{1,0:T(8,128)(2,1)S(1)}, u32[]{:S(2)}, u32[]{:S(2)}) collective-permute-start(bf16[512,256]{1,0:T(8,128)(2,1)S(1)} %product.2.refs_0_), channel_id=1, source_target_pairs={{0,1},{1,0},{2,3},{3,2},{4,5},{5,4},{6,7},{7,6},{8,9},{9,8},{10,11... | collective-permute-start | bytes 786440 | tf_op jit(solution)/shard_map/ppermute | solution.py:105
  33.2 11.5 %collective-permute-start.15 = (bf16[512,256]{1,0:T(8,128)(2,1)S(1)}, bf16[512,256]{1,0:T(8,128)(2,1)S(1)}, u32[]{:S(2)}, u32[]{:S(2)}) collective-permute-start(bf16[512,256]{1,0:T(8,128)(2,1)S(1)} %product.2.refs_0_), channel_id=1, source_target_pairs={{0,4},{1,5},{2,6},{3,7},{4,0},{5,1},{6,2},{7,3},{8,12},{9,13},{10,... | collective-permute-start | bytes 786440 | tf_op jit(solution)/shard_map/ppermute | solution.py:105
  34.7 12.6 %collective-permute-start.16 = (bf16[512,256]{1,0:T(8,128)(2,1)S(1)}, bf16[512,256]{1,0:T(8,128)(2,1)S(1)}, u32[]{:S(2)}, u32[]{:S(2)}) collective-permute-start(bf16[512,256]{1,0:T(8,128)(2,1)S(1)} %product.2.refs_0_), channel_id=1, source_target_pairs={{0,5},{1,4},{2,7},{3,6},{4,1},{5,0},{6,3},{7,2},{8,13},{9,12},{10,... | collective-permute-start | bytes 786440 | tf_op jit(solution)/shard_map/ppermute | solution.py:105
  40.2 10.1 %collective-permute-start.23 = (bf16[512,256]{1,0:T(8,128)(2,1)S(1)}, bf16[512,256]{1,0:T(8,128)(2,1)S(1)}, u32[]{:S(2)}, u32[]{:S(2)}) collective-permute-start(bf16[512,256]{1,0:T(8,128)(2,1)S(1)} %collective-permute-done.21.refs_9_), channel_id=1, source_target_pairs={{0,8},{8,0},{16,24},{24,16},{1,9},{9,1},{17,25},{25,17},{2,10},{10... | collective-permute-start | bytes 786440 | tf_op jit(solution)/shard_map/ppermute | solution.py:101
  44.1 6.1 %collective-permute-start.17 = (bf16[512,256]{1,0:T(8,128)(2,1)S(1)}, bf16[512,256]{1,0:T(8,128)(2,1)S(1)}, u32[]{:S(2)}, u32[]{:S(2)}) collective-permute-start(bf16[512,256]{1,0:T(8,128)(2,1)S(1)} %product.2.refs_0_), channel_id=1, source_target_pairs={{0,2},{2,0},{4,6},{6,4},{1,3},{3,1},{5,7},{7,5},{8,10},{10,8},{12,... | collective-permute-start | bytes 786440 | tf_op jit(solution)/shard_map/ppermute | solution.py:101
  44.1 6.1 %collective-permute-start.18 = (bf16[512,256]{1,0:T(8,128)(2,1)S(1)}, bf16[512,256]{1,0:T(8,128)(2,1)S(1)}, u32[]{:S(2)}, u32[]{:S(2)}) collective-permute-start(bf16[512,256]{1,0:T(8,128)(2,1)S(1)} %collective-permute-done.14.refs_1_), channel_id=1, source_target_pairs={{0,2},{2,0},{4,6},{6,4},{1,3},{3,1},{5,7},{7,5},{8,10},{10,8},{12,... | collective-permute-start | bytes 786440 | tf_op jit(solution)/shard_map/ppermute | solution.py:101
  44.6 5.6 %collective-permute-start.19 = (bf16[512,256]{1,0:T(8,128)(2,1)S(1)}, bf16[512,256]{1,0:T(8,128)(2,1)S(1)}, u32[]{:S(2)}, u32[]{:S(2)}) collective-permute-start(bf16[512,256]{1,0:T(8,128)(2,1)S(1)} %collective-permute-done.15.refs_2_), channel_id=1, source_target_pairs={{0,2},{2,0},{4,6},{6,4},{1,3},{3,1},{5,7},{7,5},{8,10},{10,8},{12,... | collective-permute-start | bytes 786440 | tf_op jit(solution)/shard_map/ppermute | solution.py:101
  47.2 3.0 %collective-permute-start.20 = (bf16[512,256]{1,0:T(8,128)(2,1)S(1)}, bf16[512,256]{1,0:T(8,128)(2,1)S(1)}, u32[]{:S(2)}, u32[]{:S(2)}) collective-permute-start(bf16[512,256]{1,0:T(8,128)(2,1)S(1)} %collective-permute-done.16.refs_3_), channel_id=1, source_target_pairs={{0,2},{2,0},{4,6},{6,4},{1,3},{3,1},{5,7},{7,5},{8,10},{10,8},{12,... | collective-permute-start | bytes 786440 | tf_op jit(solution)/shard_map/ppermute | solution.py:101

commit v4 on v3

--- a/solution.py
+++ b/solution.py
@@ -71,13 +71,13 @@
             for n, m in enumerate(layers):
                 at = (layer ^ m) * half + (row ^ mask) * k_rows
                 whole[pl.ds(pl.multiple_of(at, k_rows), k_rows), :] = ref[pl.ds(n * k_rows, k_rows), :]
-        total = jnp.zeros((rows, cols), jnp.float32)
-        for (masks, _), ref in zip(left, left_refs):
-            at = (layer ^ masks[1]) * half + (col ^ masks[0]) * cols
-            total += jnp.dot(
-                ref[...], whole[pl.ds(pl.multiple_of(at, cols), cols), :], preferred_element_type=jnp.float32
-            )
-        out[...] = total.astype(jnp.bfloat16)
+        at = [(layer ^ m[1]) * half + (col ^ m[0]) * cols for m, _ in left]
+        right_tiles = [whole[pl.ds(pl.multiple_of(x, cols), cols), :] for x in at]
+        out[...] = jnp.dot(
+            jnp.concatenate([ref[...] for ref in left_refs], axis=1),
+            jnp.concatenate(right_tiles, axis=0),
+            preferred_element_type=jnp.float32,
+        ).astype(jnp.bfloat16)
         if keep is not None:
             for i, j, at in blocks(keep.shape[1], keep.shape[0]):
                 out[at] = masked(out[at], rest[0][j, i])

time: 52 us -> 52 us (level)
  no operation moved by 1% of the time
where the time goes in v4:
time: 52 us; the launch traced here: 51.8 us
  waiting for transfers between devices  23.1 us (44%)
  starting transfers between devices  23 us (44%)
  Pallas kernels  3.67 us (7%)
  local copies, waits for them, and re-layouts  1.85 us (4%)
    ppermute x17, waiting for transfers between devices, exchange(): lax.ppermute(value, axes[0], [(i, i ^ mask[0]) for i in range(sizes[0])])  20.6 us
    ppermute x17, starting transfers between devices, exchange(): lax.ppermute(value, axes[0], [(i, i ^ mask[0]) for i in range(sizes[0])])  12.6 us
    ppermute x7, starting transfers between devices, exchange(): return lax.ppermute(value, axes, pairs)  10.4 us
    pallas_call x2, Pallas kernels, product(): pl.pallas_call(kernel, out_shape=jax.ShapeDtypeStruct((rows, cols), jnp.b...  2.89 us
    ppermute x7, waiting for transfers between devices, exchange(): return lax.ppermute(value, axes, pairs)  2.53 us
    transpose x1, local copies, waits for them, and re-layouts, mask_all(): h[0].transpose(1, 0, 2)  1.14 us
  transfers between devices with their start and end apart: 24, of which 10 were waited for; matrix products, arithmetic and copies ran while one was open for 0% of the time, Pallas kernels for 3%

profile of v4, /device:TPU:0, one launch (start us, length us, event | category | flops | bytes accessed | tf_op | source)
XLA Modules:
  0.0 51.8 jit_solution(3785154717574994158)
XLA Ops:
  0.0 0.0 copy-start
  0.0 1.1 %copy_bitcast_fusion = (bf16[2,256,256]{2,1,0:T(8,128)(2,1)S(1)}, bf16[2,256,256]{2,1,0:T(8,128)(2,1)S(1)}) fusion(bf16[1,256,2,256]{3,2,1,0:T(2,128)(2,1)} %param.9, bf16[1,256,2,256]{3,2,1,0:T(2,128)(2,1)} %param.8), kind=kLoop, calls=%fused_computation.1 | loop fusion | bytes 1048576 | tf_op jit(solution)/shard_map/transpose | solution.py:56
  1.1 0.0 copy-start.2
  1.2 0.0 copy-start.1
  1.2 0.0 copy-start.3
  1.2 0.0 copy-done
  1.2 0.6 %copy-done.2 = s32[1,2,2,2]{3,2,1,0:T(2,128)S(1)} copy-done((s32[1,2,2,2]{3,2,1,0:T(2,128)S(1)}, s32[1,2,2,2]{3,2,1,0:T(2,128)}, u32[]{:S(2)}) %copy-start.2) | copy-done | bytes 56
  1.8 0.0 copy-done.1
  1.9 0.0 copy-done.3
  1.9 0.8 %mask_all.1 = (bf16[512,256]{1,0:T(8,128)(2,1)S(1)}, bf16[256,256]{1,0:T(8,128)(2,1)S(1)}, bf16[256,256]{1,0:T(8,128)(2,1)S(1)}, bf16[512,256]{1,0:T(8,128)(2,1)S(1)}) custom-call(bf16[512,256]{1,0:T(8,128)(2,1)S(1)} %bitcast.16, bf16[2,256,256]{2,1,0:T(8,128)(2,1)S(1)} %get-tuple-element.28.p_ref, bf16[2,256,256]{2,1,0:T(8,128)(2,1)S(1)} %get-tuple-element.27.h_ref, ...), custom_call_target="tpu_custom_call" | custom-call | tf_op jit(solution)/shard_map/mask_all/pallas_call | solution.py:48
  2.6 3.0 %collective-permute-start = (bf16[512,256]{1,0:T(8,128)(2,1)S(1)}, bf16[512,256]{1,0:T(8,128)(2,1)S(1)}, u32[]{:S(2)}, u32[]{:S(2)}) collective-permute-start(bf16[512,256]{1,0:T(8,128)(2,1)S(1)} %get-tuple-element.19.refs_0_), channel_id=1, source_target_pairs={{0,1},{1,0},{2,3},{3,2},{4,5},{5,4},{6,7},{7,6},{8,9},{9,8},{10,11... | collective-permute-start | bytes 786440 | tf_op jit(solution)/shard_map/ppermute | solution.py:105
  5.7 3.6 %collective-permute-start.4 = (bf16[256,256]{1,0:T(8,128)(2,1)S(1)}, bf16[256,256]{1,0:T(8,128)(2,1)S(1)}, u32[]{:S(2)}, u32[]{:S(2)}) collective-permute-start(bf16[256,256]{1,0:T(8,128)(2,1)S(1)} %get-tuple-element.17.refs_8_), channel_id=1, source_target_pairs={{0,24},{8,16},{16,8},{24,0},{1,25},{9,17},{17,9},{25,1},{2,26},{10... | collective-permute-start | bytes 393224 | tf_op jit(solution)/shard_map/ppermute | solution.py:101
  9.3 0.0 collective-permute-start.1
  9.3 0.9 %collective-permute-start.9 = (bf16[256,256]{1,0:T(8,128)(2,1)S(1)}, bf16[256,256]{1,0:T(8,128)(2,1)S(1)}, u32[]{:S(2)}, u32[]{:S(2)}) collective-permute-start(bf16[256,256]{1,0:T(8,128)(2,1)S(1)} %slice.7), channel_id=1, source_target_pairs={{0,25},{1,24},{8,17},{9,16},{16,9},{17,8},{24,1},{25,0},{2,27},{3,... | collective-permute-start | bytes 393224 | tf_op jit(solution)/shard_map/ppermute | solution.py:105
  10.2 1.4 %collective-permute-start.8 = (bf16[256,256]{1,0:T(8,128)(2,1)S(1)}, bf16[256,256]{1,0:T(8,128)(2,1)S(1)}, u32[]{:S(2)}, u32[]{:S(2)}) collective-permute-start(bf16[256,256]{1,0:T(8,128)(2,1)S(1)} %slice.7), channel_id=1, source_target_pairs={{0,9},{1,8},{8,1},{9,0},{16,25},{17,24},{24,17},{25,16},{2,11},{3,... | collective-permute-start | bytes 393224 | tf_op jit(solution)/shard_map/ppermute | solution.py:105
  11.6 2.3 %collective-permute-done.4.refs_10_ = bf16[256,256]{1,0:T(8,128)(2,1)S(1)} collective-permute-done((bf16[256,256]{1,0:T(8,128)(2,1)S(1)}, bf16[256,256]{1,0:T(8,128)(2,1)S(1)}, u32[]{:S(2)}, u32[]{:S(2)}) %collective-permute-start.4) | collective-permute-done | bytes 131104 | tf_op jit(solution)/shard_map/ppermute | solution.py:101
  13.9 0.3 collective-permute-start.7
  14.2 4.4 %collective-permute-done.1.refs_11_ = bf16[256,256]{1,0:T(8,128)(2,1)S(1)} collective-permute-done((bf16[256,256]{1,0:T(8,128)(2,1)S(1)}, bf16[256,256]{1,0:T(8,128)(2,1)S(1)}, u32[]{:S(2)}, u32[]{:S(2)}) %collective-permute-start.1) | collective-permute-done | bytes 131104 | tf_op jit(solution)/shard_map/ppermute | solution.py:101
  18.6 0.0 collective-permute-done.refs_1_
  18.6 1.5 %collective-permute-start.2 = (bf16[512,256]{1,0:T(8,128)(2,1)S(1)}, bf16[512,256]{1,0:T(8,128)(2,1)S(1)}, u32[]{:S(2)}, u32[]{:S(2)}) collective-permute-start(bf16[512,256]{1,0:T(8,128)(2,1)S(1)} %get-tuple-element.19.refs_0_), channel_id=1, source_target_pairs={{0,4},{1,5},{2,6},{3,7},{4,0},{5,1},{6,2},{7,3},{8,12},{9,13},{10,... | collective-permute-start | bytes 786440 | tf_op jit(solution)/shard_map/ppermute | solution.py:105
  20.1 0.5 %collective-permute-start.3 = (bf16[512,256]{1,0:T(8,128)(2,1)S(1)}, bf16[512,256]{1,0:T(8,128)(2,1)S(1)}, u32[]{:S(2)}, u32[]{:S(2)}) collective-permute-start(bf16[512,256]{1,0:T(8,128)(2,1)S(1)} %collective-permute-done.refs_1_), channel_id=1, source_target_pairs={{0,4},{2,6},{4,0},{6,2},{1,5},{3,7},{5,1},{7,3},{8,12},{10,14},{12... | collective-permute-start | bytes 786440 | tf_op jit(solution)/shard_map/ppermute | solution.py:101
  20.6 0.0 collective-permute-done.9.refs_13_
  20.6 0.5 collective-permute-start.6
  21.1 0.0 collective-permute-done.8.refs_14_
  21.1 1.7 %collective-permute-start.10 = (bf16[256,256]{1,0:T(8,128)(2,1)S(1)}, bf16[256,256]{1,0:T(8,128)(2,1)S(1)}, u32[]{:S(2)}, u32[]{:S(2)}) collective-permute-start(bf16[256,256]{1,0:T(8,128)(2,1)S(1)} %collective-permute-done.9.refs_13_), channel_id=1, source_target_pairs={{0,8},{8,0},{16,24},{24,16},{1,9},{9,1},{17,25},{25,17},{2,10},{10... | collective-permute-start | bytes 393224 | tf_op jit(solution)/shard_map/ppermute | solution.py:101
  22.8 2.9 %collective-permute-done.6.refs_12_ = bf16[256,256]{1,0:T(8,128)(2,1)S(1)} collective-permute-done((bf16[256,256]{1,0:T(8,128)(2,1)S(1)}, bf16[256,256]{1,0:T(8,128)(2,1)S(1)}, u32[]{:S(2)}, u32[]{:S(2)}) %collective-permute-start.6) | collective-permute-done | bytes 131104 | tf_op jit(solution)/shard_map/ppermute | solution.py:101
  25.8 0.0 collective-permute-start.5
  25.8 1.4 %collective-permute-done.10.refs_15_ = bf16[256,256]{1,0:T(8,128)(2,1)S(1)} collective-permute-done((bf16[256,256]{1,0:T(8,128)(2,1)S(1)}, bf16[256,256]{1,0:T(8,128)(2,1)S(1)}, u32[]{:S(2)}, u32[]{:S(2)}) %collective-permute-start.10) | collective-permute-done | bytes 131104 | tf_op jit(solution)/shard_map/ppermute | solution.py:101
  27.2 0.0 collective-permute-done.7.refs_9_
  27.2 0.0 collective-permute-start.11
  27.2 0.0 collective-permute-done.2.refs_2_
  27.2 0.5 collective-permute-start.12
  27.7 1.4 %collective-permute-done.3.refs_3_ = bf16[512,256]{1,0:T(8,128)(2,1)S(1)} collective-permute-done((bf16[512,256]{1,0:T(8,128)(2,1)S(1)}, bf16[512,256]{1,0:T(8,128)(2,1)S(1)}, u32[]{:S(2)}, u32[]{:S(2)}) %collective-permute-start.3) | collective-permute-done | bytes 262176 | tf_op jit(solution)/shard_map/ppermute | solution.py:101
  29.1 0.0 collective-permute-start.13
  29.1 0.0 copy-start.4
  29.1 1.0 %collective-permute-start.21 = (bf16[512,256]{1,0:T(8,128)(2,1)S(1)}, bf16[512,256]{1,0:T(8,128)(2,1)S(1)}, u32[]{:S(2)}, u32[]{:S(2)}) collective-permute-start(bf16[512,256]{1,0:T(8,128)(2,1)S(1)} %pad_maximum_fusion.refs_8_), channel_id=1, source_target_pairs={{0,24},{8,16},{16,8},{24,0},{1,25},{9,17},{17,9},{25,1},{2,26},{10... | collective-permute-start | bytes 786440 | tf_op jit(solution)/shard_map/ppermute | solution.py:101
  30.1 0.0 collective-permute-done.5.refs_4_
  30.1 0.0 collective-permute-start.22
  30.1 0.0 collective-permute-done.11.refs_5_
  30.1 0.0 collective-permute-done.12.refs_6_
  30.2 0.5 collective-permute-done.13.refs_7_
  30.6 0.0 copy-done.4
  30.6 1.4 %product.2.refs_0_ = bf16[512,256]{1,0:T(8,128)(2,1)S(1)} custom-call(bf16[512,256]{1,0:T(8,128)(2,1)S(1)} %get-tuple-element.19.refs_0_, bf16[512,256]{1,0:T(8,128)(2,1)S(1)} %collective-permute-done.refs_1_, bf16[512,256]{1,0:T(8,128)(2,1)S(1)} %collective-permute-done.2.refs_2_, bf16[512,256]{1,0:T(8,128)(2,1)S(1)} %collective-permute-done.3.refs_3_, ...), custom_call_target="tpu_custom_call" | custom-call | tf_op jit(solution)/shard_map/product/pallas_call | solution.py:87
  32.0 1.1 %collective-permute-start.14 = (bf16[512,256]{1,0:T(8,128)(2,1)S(1)}, bf16[512,256]{1,0:T(8,128)(2,1)S(1)}, u32[]{:S(2)}, u32[]{:S(2)}) collective-permute-start(bf16[512,256]{1,0:T(8,128)(2,1)S(1)} %product.2.refs_0_), channel_id=1, source_target_pairs={{0,1},{1,0},{2,3},{3,2},{4,5},{5,4},{6,7},{7,6},{8,9},{9,8},{10,11... | collective-permute-start | bytes 786440 | tf_op jit(solution)/shard_map/ppermute | solution.py:105
  33.2 1.5 %collective-permute-start.15 = (bf16[512,256]{1,0:T(8,128)(2,1)S(1)}, bf16[512,256]{1,0:T(8,128)(2,1)S(1)}, u32[]{:S(2)}, u32[]{:S(2)}) collective-permute-start(bf16[512,256]{1,0:T(8,128)(2,1)S(1)} %product.2.refs_0_), channel_id=1, source_target_pairs={{0,4},{1,5},{2,6},{3,7},{4,0},{5,1},{6,2},{7,3},{8,12},{9,13},{10,... | collective-permute-start | bytes 786440 | tf_op jit(solution)/shard_map/ppermute | solution.py:105
  34.7 0.9 %collective-permute-start.16 = (bf16[512,256]{1,0:T(8,128)(2,1)S(1)}, bf16[512,256]{1,0:T(8,128)(2,1)S(1)}, u32[]{:S(2)}, u32[]{:S(2)}) collective-permute-start(bf16[512,256]{1,0:T(8,128)(2,1)S(1)} %product.2.refs_0_), channel_id=1, source_target_pairs={{0,5},{1,4},{2,7},{3,6},{4,1},{5,0},{6,3},{7,2},{8,13},{9,12},{10,... | collective-permute-start | bytes 786440 | tf_op jit(solution)/shard_map/ppermute | solution.py:105
  35.6 4.6 %collective-permute-done.21.refs_9_ = bf16[512,256]{1,0:T(8,128)(2,1)S(1)} collective-permute-done((bf16[512,256]{1,0:T(8,128)(2,1)S(1)}, bf16[512,256]{1,0:T(8,128)(2,1)S(1)}, u32[]{:S(2)}, u32[]{:S(2)}) %collective-permute-start.21) | collective-permute-done | bytes 262176 | tf_op jit(solution)/shard_map/ppermute | solution.py:101
  40.2 3.9 %collective-permute-start.23 = (bf16[512,256]{1,0:T(8,128)(2,1)S(1)}, bf16[512,256]{1,0:T(8,128)(2,1)S(1)}, u32[]{:S(2)}, u32[]{:S(2)}) collective-permute-start(bf16[512,256]{1,0:T(8,128)(2,1)S(1)} %collective-permute-done.21.refs_9_), channel_id=1, source_target_pairs={{0,8},{8,0},{16,24},{24,16},{1,9},{9,1},{17,25},{25,17},{2,10},{10... | collective-permute-start | bytes 786440 | tf_op jit(solution)/shard_map/ppermute | solution.py:101
  44.1 0.1 collective-permute-done.22.refs_10_
  44.1 0.0 collective-permute-start.17
  44.1 0.0 collective-permute-done.14.refs_1_
  44.1 0.5 collective-permute-start.18
  44.6 0.0 collective-permute-done.15.refs_2_
  44.6 0.1 collective-permute-start.19
  44.7 2.5 %collective-permute-done.16.refs_3_ = bf16[512,256]{1,0:T(8,128)(2,1)S(1)} collective-permute-done((bf16[512,256]{1,0:T(8,128)(2,1)S(1)}, bf16[512,256]{1,0:T(8,128)(2,1)S(1)}, u32[]{:S(2)}, u32[]{:S(2)}) %collective-permute-start.16) | collective-permute-done | bytes 262176 | tf_op jit(solution)/shard_map/ppermute | solution.py:105
  47.2 0.0 collective-permute-start.20
  47.2 3.0 %collective-permute-done.23.refs_11_ = bf16[512,256]{1,0:T(8,128)(2,1)S(1)} collective-permute-done((bf16[512,256]{1,0:T(8,128)(2,1)S(1)}, bf16[512,256]{1,0:T(8,128)(2,1)S(1)}, u32[]{:S(2)}, u32[]{:S(2)}) %collective-permute-start.23) | collective-permute-done | bytes 262176 | tf_op jit(solution)/shard_map/ppermute | solution.py:101
  50.3 0.0 collective-permute-done.17.refs_4_
  50.3 0.0 collective-permute-done.18.refs_5_
  50.3 0.0 collective-permute-done.19.refs_6_
  50.3 0.0 collective-permute-done.20.refs_7_
  50.3 1.5 %product.3 = bf16[512,256]{1,0:T(8,128)(2,1)} custom-call(bf16[512,256]{1,0:T(8,128)(2,1)S(1)} %product.2.refs_0_, bf16[512,256]{1,0:T(8,128)(2,1)S(1)} %collective-permute-done.14.refs_1_, bf16[512,256]{1,0:T(8,128)(2,1)S(1)} %collective-permute-done.15.refs_2_, bf16[512,256]{1,0:T(8,128)(2,1)S(1)} %collective-permute-done.16.refs_3_, ...), custom_call_target="tpu_custom_call" | custom-call | tf_op jit(solution)/shard_map/product/pallas_call | solution.py:87
  (3 shorter events, 0.0 us)
Async XLA Ops:
  0.0 1.2 %copy-start = (bf16[512,1,256]{2,0,1:T(8,128)(2,1)S(1)}, bf16[512,1,256]{2,0,1:T(8,128)(2,1)}, u32[]{:S(2)}) copy-start(bf16[512,1,256]{2,0,1:T(8,128)(2,1)} %param.7) | copy-start | bytes 786436
  1.1 0.7 %copy-start.2 = (s32[1,2,2,2]{3,2,1,0:T(2,128)S(1)}, s32[1,2,2,2]{3,2,1,0:T(2,128)}, u32[]{:S(2)}) copy-start(s32[1,2,2,2]{3,2,1,0:T(2,128)} %h_pat.1) | copy-start | bytes 100
  1.2 0.7 %copy-start.1 = (s32[1,2,2,2]{3,2,1,0:T(2,128)S(1)}, s32[1,2,2,2]{3,2,1,0:T(2,128)}, u32[]{:S(2)}) copy-start(s32[1,2,2,2]{3,2,1,0:T(2,128)} %p_pat.1) | copy-start | bytes 100
  1.2 0.7 %copy-start.3 = (s32[4,1,2]{0,2,1:T(2,128)S(1)}, s32[4,1,2]{0,2,1:T(2,128)}, u32[]{:S(2)}) copy-start(s32[4,1,2]{0,2,1:T(2,128)} %param.10) | copy-start | bytes 100
  2.6 15.9 %collective-permute-start = (bf16[512,256]{1,0:T(8,128)(2,1)S(1)}, bf16[512,256]{1,0:T(8,128)(2,1)S(1)}, u32[]{:S(2)}, u32[]{:S(2)}) collective-permute-start(bf16[512,256]{1,0:T(8,128)(2,1)S(1)} %get-tuple-element.19.refs_0_), channel_id=1, source_target_pairs={{0,1},{1,0},{2,3},{3,2},{4,5},{5,4},{6,7},{7,6},{8,9},{9,8},{10,11... | collective-permute-start | bytes 786440 | tf_op jit(solution)/shard_map/ppermute | solution.py:105
  5.7 8.2 %collective-permute-start.4 = (bf16[256,256]{1,0:T(8,128)(2,1)S(1)}, bf16[256,256]{1,0:T(8,128)(2,1)S(1)}, u32[]{:S(2)}, u32[]{:S(2)}) collective-permute-start(bf16[256,256]{1,0:T(8,128)(2,1)S(1)} %get-tuple-element.17.refs_8_), channel_id=1, source_target_pairs={{0,24},{8,16},{16,8},{24,0},{1,25},{9,17},{17,9},{25,1},{2,26},{10... | collective-permute-start | bytes 393224 | tf_op jit(solution)/shard_map/ppermute | solution.py:101
  9.3 9.3 %collective-permute-start.1 = (bf16[256,256]{1,0:T(8,128)(2,1)S(1)}, bf16[256,256]{1,0:T(8,128)(2,1)S(1)}, u32[]{:S(2)}, u32[]{:S(2)}) collective-permute-start(bf16[256,256]{1,0:T(8,128)(2,1)S(1)} %get-tuple-element.17.refs_8_), channel_id=1, source_target_pairs={{0,8},{8,0},{16,24},{24,16},{1,9},{9,1},{17,25},{25,17},{2,10},{10... | collective-permute-start | bytes 393224 | tf_op jit(solution)/shard_map/ppermute | solution.py:101
  9.3 11.3 %collective-permute-start.9 = (bf16[256,256]{1,0:T(8,128)(2,1)S(1)}, bf16[256,256]{1,0:T(8,128)(2,1)S(1)}, u32[]{:S(2)}, u32[]{:S(2)}) collective-permute-start(bf16[256,256]{1,0:T(8,128)(2,1)S(1)} %slice.7), channel_id=1, source_target_pairs={{0,25},{1,24},{8,17},{9,16},{16,9},{17,8},{24,1},{25,0},{2,27},{3,... | collective-permute-start | bytes 393224 | tf_op jit(solution)/shard_map/ppermute | solution.py:105
  10.2 10.9 %collective-permute-start.8 = (bf16[256,256]{1,0:T(8,128)(2,1)S(1)}, bf16[256,256]{1,0:T(8,128)(2,1)S(1)}, u32[]{:S(2)}, u32[]{:S(2)}) collective-permute-start(bf16[256,256]{1,0:T(8,128)(2,1)S(1)} %slice.7), channel_id=1, source_target_pairs={{0,9},{1,8},{8,1},{9,0},{16,25},{17,24},{24,17},{25,16},{2,11},{3,... | collective-permute-start | bytes 393224 | tf_op jit(solution)/shard_map/ppermute | solution.py:105
  13.9 13.3 %collective-permute-start.7 = (bf16[512,256]{1,0:T(8,128)(2,1)S(1)}, bf16[512,256]{1,0:T(8,128)(2,1)S(1)}, u32[]{:S(2)}, u32[]{:S(2)}) collective-permute-start(bf16[512,256]{1,0:T(8,128)(2,1)S(1)} %get-tuple-element.21), channel_id=1, source_target_pairs={{0,1},{1,0},{2,3},{3,2},{4,5},{5,4},{6,7},{7,6},{8,9},{9,8},{10,11... | collective-permute-start | bytes 786440 | tf_op jit(solution)/shard_map/ppermute | solution.py:101
  18.6 8.6 %collective-permute-start.2 = (bf16[512,256]{1,0:T(8,128)(2,1)S(1)}, bf16[512,256]{1,0:T(8,128)(2,1)S(1)}, u32[]{:S(2)}, u32[]{:S(2)}) collective-permute-start(bf16[512,256]{1,0:T(8,128)(2,1)S(1)} %get-tuple-element.19.refs_0_), channel_id=1, source_target_pairs={{0,4},{1,5},{2,6},{3,7},{4,0},{5,1},{6,2},{7,3},{8,12},{9,13},{10,... | collective-permute-start | bytes 786440 | tf_op jit(solution)/shard_map/ppermute | solution.py:105
  20.1 9.0 %collective-permute-start.3 = (bf16[512,256]{1,0:T(8,128)(2,1)S(1)}, bf16[512,256]{1,0:T(8,128)(2,1)S(1)}, u32[]{:S(2)}, u32[]{:S(2)}) collective-permute-start(bf16[512,256]{1,0:T(8,128)(2,1)S(1)} %collective-permute-done.refs_1_), channel_id=1, source_target_pairs={{0,4},{2,6},{4,0},{6,2},{1,5},{3,7},{5,1},{7,3},{8,12},{10,14},{12... | collective-permute-start | bytes 786440 | tf_op jit(solution)/shard_map/ppermute | solution.py:101
  20.6 5.2 %collective-permute-start.6 = (bf16[256,256]{1,0:T(8,128)(2,1)S(1)}, bf16[256,256]{1,0:T(8,128)(2,1)S(1)}, u32[]{:S(2)}, u32[]{:S(2)}) collective-permute-start(bf16[256,256]{1,0:T(8,128)(2,1)S(1)} %collective-permute-done.4.refs_10_), channel_id=1, source_target_pairs={{0,8},{8,0},{16,24},{24,16},{1,9},{9,1},{17,25},{25,17},{2,10},{10... | collective-permute-start | bytes 393224 | tf_op jit(solution)/shard_map/ppermute | solution.py:101
  21.1 6.1 %collective-permute-start.10 = (bf16[256,256]{1,0:T(8,128)(2,1)S(1)}, bf16[256,256]{1,0:T(8,128)(2,1)S(1)}, u32[]{:S(2)}, u32[]{:S(2)}) collective-permute-start(bf16[256,256]{1,0:T(8,128)(2,1)S(1)} %collective-permute-done.9.refs_13_), channel_id=1, source_target_pairs={{0,8},{8,0},{16,24},{24,16},{1,9},{9,1},{17,25},{25,17},{2,10},{10... | collective-permute-start | bytes 393224 | tf_op jit(solution)/shard_map/ppermute | solution.py:101
  25.8 4.4 %collective-permute-start.5 = (bf16[512,256]{1,0:T(8,128)(2,1)S(1)}, bf16[512,256]{1,0:T(8,128)(2,1)S(1)}, u32[]{:S(2)}, u32[]{:S(2)}) collective-permute-start(bf16[512,256]{1,0:T(8,128)(2,1)S(1)} %get-tuple-element.19.refs_0_), channel_id=1, source_target_pairs={{0,2},{2,0},{4,6},{6,4},{1,3},{3,1},{5,7},{7,5},{8,10},{10,8},{12,... | collective-permute-start | bytes 786440 | tf_op jit(solution)/shard_map/ppermute | solution.py:101
  27.2 3.0 %collective-permute-start.11 = (bf16[512,256]{1,0:T(8,128)(2,1)S(1)}, bf16[512,256]{1,0:T(8,128)(2,1)S(1)}, u32[]{:S(2)}, u32[]{:S(2)}) collective-permute-start(bf16[512,256]{1,0:T(8,128)(2,1)S(1)} %collective-permute-done.refs_1_), channel_id=1, source_target_pairs={{0,2},{2,0},{4,6},{6,4},{1,3},{3,1},{5,7},{7,5},{8,10},{10,8},{12,... | collective-permute-start | bytes 786440 | tf_op jit(solution)/shard_map/ppermute | solution.py:101
  27.2 3.0 %collective-permute-start.12 = (bf16[512,256]{1,0:T(8,128)(2,1)S(1)}, bf16[512,256]{1,0:T(8,128)(2,1)S(1)}, u32[]{:S(2)}, u32[]{:S(2)}) collective-permute-start(bf16[512,256]{1,0:T(8,128)(2,1)S(1)} %collective-permute-done.2.refs_2_), channel_id=1, source_target_pairs={{0,2},{2,0},{4,6},{6,4},{1,3},{3,1},{5,7},{7,5},{8,10},{10,8},{12,... | collective-permute-start | bytes 786440 | tf_op jit(solution)/shard_map/ppermute | solution.py:101
  29.1 1.5 %collective-permute-start.13 = (bf16[512,256]{1,0:T(8,128)(2,1)S(1)}, bf16[512,256]{1,0:T(8,128)(2,1)S(1)}, u32[]{:S(2)}, u32[]{:S(2)}) collective-permute-start(bf16[512,256]{1,0:T(8,128)(2,1)S(1)} %collective-permute-done.3.refs_3_), channel_id=1, source_target_pairs={{0,2},{2,0},{4,6},{6,4},{1,3},{3,1},{5,7},{7,5},{8,10},{10,8},{12,... | collective-permute-start | bytes 786440 | tf_op jit(solution)/shard_map/ppermute | solution.py:101
  29.1 1.5 %copy-start.4 = (s32[4,1,2]{0,2,1:T(2,128)S(1)}, s32[4,1,2]{0,2,1:T(2,128)}, u32[]{:S(2)}) copy-start(s32[4,1,2]{0,2,1:T(2,128)} %param.13) | copy-start | bytes 100
  29.1 11.0 %collective-permute-start.21 = (bf16[512,256]{1,0:T(8,128)(2,1)S(1)}, bf16[512,256]{1,0:T(8,128)(2,1)S(1)}, u32[]{:S(2)}, u32[]{:S(2)}) collective-permute-start(bf16[512,256]{1,0:T(8,128)(2,1)S(1)} %pad_maximum_fusion.refs_8_), channel_id=1, source_target_pairs={{0,24},{8,16},{16,8},{24,0},{1,25},{9,17},{17,9},{25,1},{2,26},{10... | collective-permute-start | bytes 786440 | tf_op jit(solution)/shard_map/ppermute | solution.py:101
  30.1 14.0 %collective-permute-start.22 = (bf16[512,256]{1,0:T(8,128)(2,1)S(1)}, bf16[512,256]{1,0:T(8,128)(2,1)S(1)}, u32[]{:S(2)}, u32[]{:S(2)}) collective-permute-start(bf16[512,256]{1,0:T(8,128)(2,1)S(1)} %pad_maximum_fusion.refs_8_), channel_id=1, source_target_pairs={{0,8},{8,0},{16,24},{24,16},{1,9},{9,1},{17,25},{25,17},{2,10},{10... | collective-permute-start | bytes 786440 | tf_op jit(solution)/shard_map/ppermute | solution.py:101
  32.0 12.1 %collective-permute-start.14 = (bf16[512,256]{1,0:T(8,128)(2,1)S(1)}, bf16[512,256]{1,0:T(8,128)(2,1)S(1)}, u32[]{:S(2)}, u32[]{:S(2)}) collective-permute-start(bf16[512,256]{1,0:T(8,128)(2,1)S(1)} %product.2.refs_0_), channel_id=1, source_target_pairs={{0,1},{1,0},{2,3},{3,2},{4,5},{5,4},{6,7},{7,6},{8,9},{9,8},{10,11... | collective-permute-start | bytes 786440 | tf_op jit(solution)/shard_map/ppermute | solution.py:105
  33.2 11.5 %collective-permute-start.15 = (bf16[512,256]{1,0:T(8,128)(2,1)S(1)}, bf16[512,256]{1,0:T(8,128)(2,1)S(1)}, u32[]{:S(2)}, u32[]{:S(2)}) collective-permute-start(bf16[512,256]{1,0:T(8,128)(2,1)S(1)} %product.2.refs_0_), channel_id=1, source_target_pairs={{0,4},{1,5},{2,6},{3,7},{4,0},{5,1},{6,2},{7,3},{8,12},{9,13},{10,... | collective-permute-start | bytes 786440 | tf_op jit(solution)/shard_map/ppermute | solution.py:105
  34.7 12.6 %collective-permute-start.16 = (bf16[512,256]{1,0:T(8,128)(2,1)S(1)}, bf16[512,256]{1,0:T(8,128)(2,1)S(1)}, u32[]{:S(2)}, u32[]{:S(2)}) collective-permute-start(bf16[512,256]{1,0:T(8,128)(2,1)S(1)} %product.2.refs_0_), channel_id=1, source_target_pairs={{0,5},{1,4},{2,7},{3,6},{4,1},{5,0},{6,3},{7,2},{8,13},{9,12},{10,... | collective-permute-start | bytes 786440 | tf_op jit(solution)/shard_map/ppermute | solution.py:105
  40.2 10.1 %collective-permute-start.23 = (bf16[512,256]{1,0:T(8,128)(2,1)S(1)}, bf16[512,256]{1,0:T(8,128)(2,1)S(1)}, u32[]{:S(2)}, u32[]{:S(2)}) collective-permute-start(bf16[512,256]{1,0:T(8,128)(2,1)S(1)} %collective-permute-done.21.refs_9_), channel_id=1, source_target_pairs={{0,8},{8,0},{16,24},{24,16},{1,9},{9,1},{17,25},{25,17},{2,10},{10... | collective-permute-start | bytes 786440 | tf_op jit(solution)/shard_map/ppermute | solution.py:101
  44.1 6.1 %collective-permute-start.17 = (bf16[512,256]{1,0:T(8,128)(2,1)S(1)}, bf16[512,256]{1,0:T(8,128)(2,1)S(1)}, u32[]{:S(2)}, u32[]{:S(2)}) collective-permute-start(bf16[512,256]{1,0:T(8,128)(2,1)S(1)} %product.2.refs_0_), channel_id=1, source_target_pairs={{0,2},{2,0},{4,6},{6,4},{1,3},{3,1},{5,7},{7,5},{8,10},{10,8},{12,... | collective-permute-start | bytes 786440 | tf_op jit(solution)/shard_map/ppermute | solution.py:101
  44.1 6.1 %collective-permute-start.18 = (bf16[512,256]{1,0:T(8,128)(2,1)S(1)}, bf16[512,256]{1,0:T(8,128)(2,1)S(1)}, u32[]{:S(2)}, u32[]{:S(2)}) collective-permute-start(bf16[512,256]{1,0:T(8,128)(2,1)S(1)} %collective-permute-done.14.refs_1_), channel_id=1, source_target_pairs={{0,2},{2,0},{4,6},{6,4},{1,3},{3,1},{5,7},{7,5},{8,10},{10,8},{12,... | collective-permute-start | bytes 786440 | tf_op jit(solution)/shard_map/ppermute | solution.py:101
  44.6 5.6 %collective-permute-start.19 = (bf16[512,256]{1,0:T(8,128)(2,1)S(1)}, bf16[512,256]{1,0:T(8,128)(2,1)S(1)}, u32[]{:S(2)}, u32[]{:S(2)}) collective-permute-start(bf16[512,256]{1,0:T(8,128)(2,1)S(1)} %collective-permute-done.15.refs_2_), channel_id=1, source_target_pairs={{0,2},{2,0},{4,6},{6,4},{1,3},{3,1},{5,7},{7,5},{8,10},{10,8},{12,... | collective-permute-start | bytes 786440 | tf_op jit(solution)/shard_map/ppermute | solution.py:101
  47.2 3.0 %collective-permute-start.20 = (bf16[512,256]{1,0:T(8,128)(2,1)S(1)}, bf16[512,256]{1,0:T(8,128)(2,1)S(1)}, u32[]{:S(2)}, u32[]{:S(2)}) collective-permute-start(bf16[512,256]{1,0:T(8,128)(2,1)S(1)} %collective-permute-done.16.refs_3_), channel_id=1, source_target_pairs={{0,2},{2,0},{4,6},{6,4},{1,3},{3,1},{5,7},{7,5},{8,10},{10,8},{12,... | collective-permute-start | bytes 786440 | tf_op jit(solution)/shard_map/ppermute | solution.py:101
